TPU v7x, 32 devices: a whole 2x2x4 slice. The times are simulated.
32 devices in a mesh: grp: 1, seq: 8 (over z, y), head: 4 (over x, core).
Axes of the slice: x: 2, y: 2, z: 4, core: 2. Of those that a mesh axis runs over, the one named last changes fastest.
Arguments:
- ssm_values: bfloat16 [2048, 4096], P(('grp', 'seq'), 'head'), may hold values from -6 to 6
- ssm_gate: bfloat16 [2048, 4096], P(('grp', 'seq'), 'head'), may hold values from -6 to 6
- write_proj: bfloat16 [2048, 1024], P(('grp', 'seq'), 'head'), may hold values from -2.5 to 2.5
- read_proj: bfloat16 [2048, 1024], P(('grp', 'seq'), 'head'), may hold values from -2.5 to 2.5
- step_size: float32 [2048, 64], P(('grp', 'seq'), 'head'), may hold values from 0.003125 to 0.2
- decay_power: int32 [64], P('head'), may hold values from 0 to 15
- skip_gain: float32 [64], P('head'), may hold values from 0.5 to 1.5
- norm_gain: float32 [4096], P('head'), may hold values from 0.1 to 1.9
- out_weight: bfloat16 [4096, 2688], P('head', 'seq'), may hold values from -0.09375 to 0.09375
- residual: bfloat16 [2048, 2688], P(('grp', 'seq', 'head')), may hold values from -6 to 6
- expert_norm: float32 [2688], replicated, may hold values from 0.1 to 1.9
- router_weight: bfloat16 [2688, 16], replicated, may hold values from -0.125 to 0.125
- expert_index: int32 [2048, 6], P(('grp', 'seq', 'head')), may hold values from 0 to 15, all different within a row; in each aligned block of 64 rows (0 to 63, 64 to 127, ...) at most 32 rows name the same one
- up_weight: bfloat16 [32, 2688, 928], P(('seq', 'head')), may hold values from -0.125 to 0.125
- down_weight: bfloat16 [32, 928, 2688], P(('seq', 'head')), may hold values from -0.125 to 0.125
Outputs:
- layer_out: bfloat16 [2048, 2688], P(('grp', 'seq', 'head'))
Inputs may be any that keep to these rules, and one draw needn't show every extreme that they name: `expert_index`: each row names 6 different experts. In the rows of one device (aligned blocks of 64 rows) no expert is named more than 32 times, a bound that some block reaches.
All inputs are finite; a program needn't handle non-finite values.
Results may differ from a plain program's by a relative error of at most 0.019.
Values may be sent and summed in bfloat16 or wider, within the bound.
No kernel may reach another device: no remote copies, remote signals or barrier semaphores. Data moves between devices by JAX's collectives and lax.ppermute only.
A program may use at most 64 MiB of HBM per device.

v0:
```python
import jax
import jax.numpy as jnp
from jax import lax
from jax.sharding import PartitionSpec as P


HEADS = 64
HEAD_DIM = 64
STATE = 128
GROUPS = 8
TOP = 6
BLOCK_LEN = 256


EPSILON = 1e-05
ROUTE_SCALE = 2.5


def seq_ring(size):
    return list(range(0, size, 2)) + list(range(1, size, 2))[::-1]


def shift(x, axis, order, step):
    size = len(order)
    return lax.ppermute(x, axis, [(order[i], order[(i + step) % size]) for i in range(size)])


def pick(parts, index):
    return lax.dynamic_index_in_dim(parts, index, 0, keepdims=False)


def packed(state, decay):
    high = decay.astype(jnp.bfloat16)
    low = (decay - high.astype(jnp.float32)).astype(jnp.bfloat16)
    rows = jnp.zeros((16, STATE), jnp.bfloat16)
    rows = rows.at[0, : decay.shape[0]].set(high).at[1, : decay.shape[0]].set(low)
    return jnp.concatenate([state.reshape(-1, STATE).astype(jnp.bfloat16), rows], axis=0)


def unpacked(block, heads):
    rows = heads * HEAD_DIM
    state = block[:rows].astype(jnp.float32).reshape(heads, HEAD_DIM, STATE)
    decay = block[rows, :heads].astype(jnp.float32) + block[rows + 1, :heads].astype(jnp.float32)
    return state, decay


def swapped(decay, state, axis):
    size, side = lax.axis_size(axis), lax.axis_index(axis) % 2
    half = decay.shape[0] // 2
    states = state.reshape(2, half, HEAD_DIM, STATE)
    decays = decay.reshape(2, half)
    return lax.ppermute(
        packed(pick(states, 1 - side), pick(decays, 1 - side)),
        axis,
        [(i, i ^ 1) for i in range(size)],
    )


def entering(got, decay, state, axis):
    size, side = lax.axis_size(axis), lax.axis_index(axis) % 2
    odd = side == 1
    half = decay.shape[0] // 2
    other_state, other_decay = unpacked(got, half)
    own_state = pick(state.reshape(2, half, HEAD_DIM, STATE), side)
    own_decay = pick(decay.reshape(2, half), side)
    first_state = jnp.where(odd, other_state, own_state)
    second_state = jnp.where(odd, own_state, other_state)
    first_decay = jnp.where(odd, other_decay, own_decay)
    second_decay = jnp.where(odd, own_decay, other_decay)
    pair = packed(
        second_decay[:, None, None] * first_state + second_state, first_decay * second_decay
    )
    before = jnp.zeros_like(first_state)
    received = [
        lax.ppermute(pair, axis, [(i, i + 2 * d) for i in range(size - 2 * d)])
        for d in range(1, size // 2)
    ]
    for block in received[::-1]:
        block_state, block_decay = unpacked(block, half)
        before = block_decay[:, None, None] * before + block_state
    inner = first_decay[:, None, None] * before + first_state
    mine_half = jnp.where(odd, inner, before)
    send_half = jnp.where(odd, before, inner).astype(jnp.bfloat16)
    back = lax.ppermute(
        send_half.reshape(-1, STATE), axis, [(i, i ^ 1) for i in range(size)]
    )
    back = back.astype(jnp.float32).reshape(mine_half.shape)
    low = jnp.where(odd, back, mine_half)
    high = jnp.where(odd, mine_half, back)
    return jnp.concatenate([low, high], axis=0)


def ring_step(parts, axis, step):
    size = lax.axis_size(axis)
    order = seq_ring(size)
    ahead, behind = parts
    if 2 * step < size:
        ahead = tuple(shift(part, axis, order, 1) for part in ahead)
        behind = tuple(shift(part, axis, order, -1) for part in behind)
        return ahead, behind
    return (shift(ahead[0], axis, order, 1),), (shift(behind[1], axis, order, -1),)


def head_scatter(pieces, axis):
    size, mine = lax.axis_size(axis), lax.axis_index(axis)
    stride = 1
    while stride < size:
        bit = (mine // stride) % 2
        left = pieces.shape[0] // 2
        view = pieces.reshape(left, 2, *pieces.shape[1:])
        send = lax.dynamic_index_in_dim(view, 1 - bit, 1, keepdims=False)
        keep = lax.dynamic_index_in_dim(view, bit, 1, keepdims=False)
        came = lax.ppermute(send, axis, [(i, i ^ stride) for i in range(size)])
        pieces = (keep.astype(jnp.float32) + came.astype(jnp.float32)).astype(jnp.bfloat16)
        stride *= 2
    return pieces[0]


def across(x, mask):
    axes = ("seq", "head")
    return lax.ppermute(x, axes, [(i, i ^ mask) for i in range(lax.axis_size(axes))])


def expert_half(slot_rows, up_weight, down_weight):
    model_width = slot_rows.shape[-1]
    flat_rows = slot_rows.reshape(-1, model_width)
    activation = jnp.dot(flat_rows, up_weight[0], preferred_element_type=jnp.float32)
    activation = jnp.maximum(activation, 0.0)
    activation = (activation * activation).astype(jnp.bfloat16)
    output = jnp.dot(activation, down_weight[0], preferred_element_type=jnp.float32).astype(
        jnp.bfloat16
    )
    return output.reshape(slot_rows.shape)


def per_device(
    ssm_values,
    ssm_gate,
    write_proj,
    read_proj,
    step_size,
    decay_power,
    skip_gain,
    norm_gain,
    out_weight,
    residual,
    expert_norm,
    router_weight,
    expert_index,
    up_weight,
    down_weight,
):
    tokens_dev = ssm_values.shape[0]
    heads_dev = step_size.shape[1]
    per_group = HEADS // GROUPS
    groups_dev = heads_dev // per_group
    count_blocks = tokens_dev // BLOCK_LEN
    seq_size = lax.axis_size("seq")
    head_size = lax.axis_size("head")
    shard = out_weight.T
    cut = (shard.shape[0] // 2 + 15) // 16 * 16
    halves = (shard[:cut], shard[cut:])
    ring = [ring_step((halves, halves), "seq", 1)]
    decay_rates = jnp.exp2(-decay_power.astype(jnp.float32))
    values = ssm_values.reshape(count_blocks, BLOCK_LEN, heads_dev, HEAD_DIM)
    steps_all = step_size.reshape(count_blocks, BLOCK_LEN, heads_dev)
    writes = write_proj.reshape(count_blocks, BLOCK_LEN, groups_dev, STATE)
    reads = read_proj.reshape(count_blocks, BLOCK_LEN, groups_dev, STATE)
    causal = jnp.tril(jnp.ones((BLOCK_LEN, BLOCK_LEN), dtype=bool))

    def one_block(pieces):
        values_in, steps_in, write_in, read_in = pieces
        log_decay = -steps_in * decay_rates[None, :]
        cumulative = jnp.cumsum(log_decay, axis=0)
        scores = jnp.einsum("tgn,sgn->gts", read_in, write_in, preferred_element_type=jnp.float32)
        scores = jnp.repeat(scores, per_group, axis=0)
        decays = jnp.exp(cumulative.T[:, :, None] - cumulative.T[:, None, :])
        mixing = jnp.where(causal[None], scores * decays * steps_in.T[:, None, :], 0.0).astype(
            jnp.bfloat16
        )
        inner_out = jnp.einsum(
            "hts,shp->thp", mixing, values_in, preferred_element_type=jnp.float32
        )
        block_total = cumulative[-1]
        weighted = (
            values_in.astype(jnp.float32)
            * (jnp.exp(block_total[None, :] - cumulative) * steps_in)[:, :, None]
        ).astype(jnp.bfloat16)
        write_heads = jnp.repeat(write_in, per_group, axis=1)
        fresh_state = jnp.einsum(
            "shp,shn->hpn", weighted, write_heads, preferred_element_type=jnp.float32
        )
        return (inner_out, fresh_state, block_total, cumulative)

    inner_all, fresh_all, totals_blk, cumul_all = lax.map(
        one_block, (values, steps_all, writes, reads)
    )

    def summarize(carried_in, pieces):
        decay_prod, summary = carried_in
        block_total, fresh_state = pieces
        factor = jnp.exp(block_total)
        return ((decay_prod * factor, factor[:, None, None] * summary + fresh_state), None)

    zero_state = jnp.zeros((heads_dev, HEAD_DIM, STATE), jnp.float32)
    (device_decay, device_state), unused = lax.scan(
        summarize, (jnp.ones((heads_dev,), jnp.float32), zero_state), (totals_blk, fresh_all)
    )

    got = swapped(device_decay, device_state, "seq")
    ring[0], got = lax.optimization_barrier((ring[0], got))
    for step in range(2, seq_size // 2 + 1):
        ring.append(ring_step(ring[-1], "seq", step))
    incoming = entering(got, device_decay, device_state, "seq")

    def emit_rows(carry_state, pieces):
        read_in, cumulative, block_total, fresh_state = pieces
        read_heads = jnp.repeat(read_in, per_group, axis=1)
        carried = jnp.einsum(
            "thn,hpn->thp",
            read_heads,
            carry_state.astype(jnp.bfloat16),
            preferred_element_type=jnp.float32,
        )
        carried = carried * jnp.exp(cumulative)[:, :, None]
        return (jnp.exp(block_total)[:, None, None] * carry_state + fresh_state, carried)

    _, carried_all = lax.scan(emit_rows, incoming, (reads, cumul_all, totals_blk, fresh_all))
    values_flat = ssm_values.reshape(tokens_dev, heads_dev, HEAD_DIM).astype(jnp.float32)
    ssm_out = (inner_all + carried_all).reshape(tokens_dev, heads_dev, HEAD_DIM) + skip_gain[
        None, :, None
    ] * values_flat
    gate_vals = ssm_gate.reshape(tokens_dev, heads_dev, HEAD_DIM).astype(jnp.float32)
    gated = (ssm_out * jax.nn.silu(gate_vals)).reshape(tokens_dev, groups_dev, per_group * HEAD_DIM)
    inv_rms = lax.rsqrt(jnp.mean(gated * gated, axis=-1, keepdims=True) + EPSILON)
    normed = (
        (gated * inv_rms).reshape(tokens_dev, heads_dev * HEAD_DIM) * norm_gain[None, :]
    ).astype(jnp.bfloat16)
    rows_own = tokens_dev // head_size
    shard_width = out_weight.shape[1]

    def product(parts):
        rows = parts[0] if len(parts) == 1 else jnp.concatenate(parts, axis=0)
        result = lax.dot_general(
            normed, rows, (((1,), (1,)), ((), ())), preferred_element_type=jnp.float32
        ).astype(jnp.bfloat16)
        return [
            result[:, at : at + shard_width].reshape(head_size, 1, rows_own, shard_width)
            for at in range(0, result.shape[1], shard_width)
        ]

    offsets, products = [0], product([shard])
    batches = []
    for step in range(1, seq_size // 2 + 1):
        ahead, behind = ring[step - 1]
        offsets += [-step, step] if 2 * step < seq_size else [-step]
        products += product([*ahead, *behind])
        if step in (seq_size // 4, seq_size // 2):
            batches.append(head_scatter(jnp.concatenate(products, axis=1), "head"))
            products = []
    scattered = jnp.concatenate(batches, axis=0).astype(jnp.float32)
    order = seq_ring(seq_size)
    table = [[0] * seq_size for _ in range(seq_size)]
    for place, index in enumerate(order):
        for at, step in enumerate(offsets):
            table[index][order[(place + step) % seq_size]] = at
    places = jnp.asarray(table, jnp.int32)[lax.axis_index("seq")]
    mixed_out = jnp.concatenate(
        [pick(scattered, places[b]) for b in range(seq_size)], axis=1
    )
    hidden = residual.astype(jnp.float32) + mixed_out
    inputs = (
        hidden
        * lax.rsqrt(jnp.mean(hidden * hidden, axis=-1, keepdims=True) + EPSILON)
        * expert_norm[None, :]
    ).astype(jnp.bfloat16)
    logits = jnp.dot(inputs, router_weight, preferred_element_type=jnp.float32)
    experts = router_weight.shape[1]
    model_width = inputs.shape[1]
    expert_hits = expert_index[:, :, None] == jnp.arange(experts, dtype=jnp.int32)[None, None, :]
    picked = jnp.sum(jnp.where(expert_hits, logits[:, None, :], 0.0), axis=-1)
    probability = jax.nn.sigmoid(picked)
    shares = ROUTE_SCALE * probability / jnp.sum(probability, axis=1, keepdims=True)
    flat_hits = expert_hits.astype(jnp.int32).reshape(rows_own * TOP, experts)
    before = jnp.cumsum(flat_hits, axis=0) - flat_hits
    slot_index = jnp.sum(before * flat_hits, axis=1).reshape(rows_own, TOP)
    capacity = 8 * TOP * tokens_dev // (3 * seq_size * head_size * head_size)
    notes = jnp.concatenate(
        [expert_index.astype(jnp.bfloat16), slot_index.astype(jnp.bfloat16), shares.astype(jnp.bfloat16)],
        axis=1,
    )
    notes = jnp.pad(notes, ((0, 0), (0, 128 - notes.shape[1])))
    moe_out = routed(
        jnp.concatenate([inputs, notes], axis=1), model_width, capacity, experts, up_weight, down_weight
    )
    return (hidden + moe_out).astype(jnp.bfloat16)


def routed(block, width, capacity, experts, up_weight, down_weight):
    inner = experts // 4
    stride = 2 * inner
    place = lax.axis_index("seq") * lax.axis_size("head") + lax.axis_index("head")
    mine_outer, mine_inner = place // stride, place // 2 % inner
    turned = mine_inner ^ jnp.arange(inner, dtype=jnp.int32)
    wanted = (mine_outer * inner + turned)[:, None] * capacity + jnp.arange(capacity, dtype=jnp.int32)
    wanted = wanted.reshape(-1).astype(jnp.float32)

    def placed(rows):
        notes = rows[:, width : width + 3 * TOP].astype(jnp.float32)
        code = notes[:, :TOP] * capacity + notes[:, TOP : 2 * TOP]
        match = code[:, :, None] == wanted[None, None, :]
        placing = jnp.any(match, axis=1).astype(jnp.bfloat16)
        weights = jnp.sum(jnp.where(match, notes[:, 2 * TOP :, None], 0.0), axis=1)
        return placing, weights.astype(jnp.bfloat16)

    def spread(rows):
        placing, weights = placed(rows)
        inputs = rows[:, :width]
        parts = []
        for m in range(inner):
            part = lax.dot_general(
                placing[:, m * capacity : (m + 1) * capacity],
                inputs,
                (((0,), (0,)), ((), ())),
                preferred_element_type=jnp.float32,
            ).astype(jnp.bfloat16)
            parts.append(across(part, 2 * m) if m else part)
        return parts, weights

    def expert(parts):
        own_rows = jnp.concatenate(parts, axis=0)
        other_rows = across(own_rows, 1)
        rows = jnp.concatenate([own_rows, other_rows], axis=0)
        both = expert_half(rows, up_weight, down_weight)
        half = own_rows.shape[0]
        back = across(both[half:], 1)
        return (both[:half].astype(jnp.float32) + back.astype(jnp.float32)).astype(jnp.bfloat16)

    def brought(summed):
        results = []
        for m in range(inner):
            part = summed[m * capacity : (m + 1) * capacity]
            results.append(across(part, 2 * m) if m else part)
        return results

    def home(results, weights, k):
        partial = jnp.dot(
            weights, jnp.concatenate(results, axis=0), preferred_element_type=jnp.float32
        )
        return across(partial.astype(jnp.bfloat16), k * stride) if k else partial

    def line(k):
        return across(block, k * stride)

    rows1 = line(1)
    sent0 = spread(block)
    rows1, sent0, block = lax.optimization_barrier((rows1, sent0, block))

    rows2 = line(2)
    sent1 = spread(rows1)
    done0 = expert(sent0[0])
    rows2, sent1, done0, block = lax.optimization_barrier((rows2, sent1, done0, block))

    rows3 = line(3)
    sent2 = spread(rows2)
    done1 = expert(sent1[0])
    back0 = brought(done0)
    rows3, sent2, done1, back0 = lax.optimization_barrier((rows3, sent2, done1, back0))

    sent3 = spread(rows3)
    done2 = expert(sent2[0])
    back1 = brought(done1)
    sum0 = home(back0, sent0[1], 0)
    sent3, done2, back1, sum0 = lax.optimization_barrier((sent3, done2, back1, sum0))

    done3 = expert(sent3[0])
    back2 = brought(done2)
    sum1 = home(back1, sent1[1], 1)
    back3 = brought(done3)
    sum2 = home(back2, sent2[1], 2)
    sum3 = home(back3, sent3[1], 3)
    total = sum0
    for part in (sum1, sum2, sum3):
        total = total + part.astype(jnp.float32)
    return total


def solution(mesh):
    return jax.shard_map(
        per_device,
        mesh=mesh,
        in_specs=(
            P(("grp", "seq"), "head"),
            P(("grp", "seq"), "head"),
            P(("grp", "seq"), "head"),
            P(("grp", "seq"), "head"),
            P(("grp", "seq"), "head"),
            P("head"),
            P("head"),
            P("head"),
            P("head", "seq"),
            P(("grp", "seq", "head"), None),
            P(),
            P(),
            P(("grp", "seq", "head"), None),
            P(("seq", "head"), None, None),
            P(("seq", "head"), None, None),
        ),
        out_specs=P(("grp", "seq", "head"), None),
        check_vma=False,
    )
```

profile of v0, /device:TPU:9, one launch (start us, length us, event | category | flops | bytes accessed | tf_op | source)
XLA Modules:
  0.0 264.1 jit_solution(2057483057984926274)
XLA Ops:
  10.8 1.8 convolution_bitcast_fusion
  32.7 3.2 %collective-permute-start.5 = (bf16[528,128]{1,0:T(8,128)(2,1)S(1)}, bf16[528,128]{1,0:T(8,128)(2,1)S(1)}, u32[]{:S(2)}, u32[]{:S(2)}) collective-permute-start(bf16[528,128]{1,0:T(8,128)(2,1)S(1)} %pad_maximum_fusion.6), channel_id=1, source_target_pairs={{0,8},{4,12},{8,16},{12,20},{16,24},{20,28},{1,9},{5,13},{9,17},{1... | collective-permute-start | bytes 405512 | tf_op jit(solution)/shard_map/ppermute | solution.py:75
  35.9 2.3 collective-permute-start.6
  39.1 2.7 %collective-permute-start.11 = (bf16[176,1024]{1,0:T(8,128)(2,1)}, bf16[176,1024]{1,0:T(8,128)(2,1)}, u32[]{:S(2)}, u32[]{:S(2)}) collective-permute-start(bf16[176,1024]{1,0:T(8,128)(2,1)} %collective-permute-done.2), channel_id=1, source_target_pairs={{0,4},{8,0},{16,8},{24,16},{28,24},{20,28},{12,20},{4,12},{1,5},{9... | collective-permute-start | bytes 1081352 | tf_op jit(solution)/shard_map/ppermute | solution.py:25
  42.1 2.9 %collective-permute-done.6 = bf16[528,128]{1,0:T(8,128)(2,1)S(1)} collective-permute-done((bf16[528,128]{1,0:T(8,128)(2,1)S(1)}, bf16[528,128]{1,0:T(8,128)(2,1)S(1)}, u32[]{:S(2)}, u32[]{:S(2)}) %collective-permute-start.6) | collective-permute-done | bytes 135200 | tf_op jit(solution)/shard_map/ppermute | solution.py:75
  45.9 4.0 %collective-permute-done.8 = bf16[512,128]{1,0:T(8,128)(2,1)S(1)} collective-permute-done((bf16[512,128]{1,0:T(8,128)(2,1)S(1)}, bf16[512,128]{1,0:T(8,128)(2,1)S(1)}, u32[]{:S(2)}, u32[]{:S(2)}) %collective-permute-start.8) | collective-permute-done | bytes 131104 | tf_op jit(solution)/shard_map/ppermute | solution.py:84
  51.4 1.7 fusion.106
  53.9 1.6 copy.182
  56.0 2.1 fusion.99
  59.2 2.9 %collective-permute-done.10 = bf16[160,1024]{1,0:T(8,128)(2,1)} collective-permute-done((bf16[160,1024]{1,0:T(8,128)(2,1)}, bf16[160,1024]{1,0:T(8,128)(2,1)}, u32[]{:S(2)}, u32[]{:S(2)}) %collective-permute-start.10) | collective-permute-done | bytes 327712 | tf_op jit(solution)/shard_map/ppermute | solution.py:25
  62.1 2.2 collective-permute-start.16
  64.3 4.3 %collective-permute-start.18 = (bf16[160,1024]{1,0:T(8,128)(2,1)}, bf16[160,1024]{1,0:T(8,128)(2,1)}, u32[]{:S(2)}, u32[]{:S(2)}) collective-permute-start(bf16[160,1024]{1,0:T(8,128)(2,1)} %collective-permute-done.12), channel_id=1, source_target_pairs={{0,4},{8,0},{16,8},{24,16},{28,24},{20,28},{12,20},{4,12},{1,5},{9... | collective-permute-start | bytes 983048 | tf_op jit(solution)/shard_map/ppermute | solution.py:25
  68.7 1.9 fusion.96
  72.5 4.6 %collective-permute-start.13 = (bf16[2,5,64,336]{3,2,0,1:T(8,128)(2,1)S(1)}, bf16[2,5,64,336]{3,2,0,1:T(8,128)(2,1)S(1)}, u32[]{:S(2)}, u32[]{:S(2)}) collective-permute-start(bf16[2,5,64,336]{3,2,0,1:T(8,128)(2,1)S(1)} %dynamic-slice_bitcast_fusion), channel_id=1, source_target_pairs={{0,1},{1,0},{2,3},{3,2},{4,5},{5,4},{6,7},{7,6},{8,9},{9,8},{10,11... | collective-permute-start | bytes 1290248 | tf_op jit(solution)/shard_map/ppermute | solution.py:113
  77.1 1.7 collective-permute-start.20
  78.8 2.2 collective-permute-done.15
  81.0 1.9 fusion.93
  83.3 4.2 %collective-permute-done.20 = bf16[160,1024]{1,0:T(8,128)(2,1)} collective-permute-done((bf16[160,1024]{1,0:T(8,128)(2,1)}, bf16[160,1024]{1,0:T(8,128)(2,1)}, u32[]{:S(2)}, u32[]{:S(2)}) %collective-permute-start.20) | collective-permute-done | bytes 327712 | tf_op jit(solution)/shard_map/ppermute | solution.py:25
  90.6 5.2 %collective-permute-start.21 = (bf16[2,3,64,336]{3,2,1,0:T(8,128)(2,1)S(1)}, bf16[2,3,64,336]{3,2,1,0:T(8,128)(2,1)S(1)}, u32[]{:S(2)}, u32[]{:S(2)}) collective-permute-start(bf16[2,3,64,336]{3,2,1,0:T(8,128)(2,1)S(1)} %bitcast.281), channel_id=1, source_target_pairs={{0,1},{1,0},{2,3},{3,2},{4,5},{5,4},{6,7},{7,6},{8,9},{9,8},{10,11... | collective-permute-start | bytes 774152 | tf_op jit(solution)/shard_map/ppermute | solution.py:113
  98.4 5.1 %collective-permute-done.14 = bf16[1,5,64,336]{3,2,0,1:T(8,128)(2,1)S(1)} collective-permute-done((bf16[1,5,64,336]{3,2,0,1:T(8,128)(2,1)S(1)}, bf16[1,5,64,336]{3,2,0,1:T(8,128)(2,1)S(1)}, u32[]{:S(2)}, u32[]{:S(2)}) %collective-permute-start.14) | collective-permute-done | bytes 215072 | tf_op jit(solution)/shard_map/ppermute | solution.py:113
  103.6 3.1 %collective-permute-done.22 = bf16[1,3,64,336]{3,2,1,0:T(8,128)(2,1)S(1)} collective-permute-done((bf16[1,3,64,336]{3,2,1,0:T(8,128)(2,1)S(1)}, bf16[1,3,64,336]{3,2,1,0:T(8,128)(2,1)S(1)}, u32[]{:S(2)}, u32[]{:S(2)}) %collective-permute-start.22) | collective-permute-done | bytes 129056 | tf_op jit(solution)/shard_map/ppermute | solution.py:113
  109.9 1.8 collective-permute-start.23
  115.2 2.7 %collective-permute-done.26 = bf16[32,2688]{1,0:T(8,128)(2,1)S(1)} collective-permute-done((bf16[32,2688]{1,0:T(8,128)(2,1)S(1)}, bf16[32,2688]{1,0:T(8,128)(2,1)S(1)}, u32[]{:S(2)}, u32[]{:S(2)}) %collective-permute-start.26) | collective-permute-done | bytes 172064 | tf_op jit(solution)/shard_map/ppermute | solution.py:121
  117.8 5.2 %collective-permute-done.25 = bf16[32,2688]{1,0:T(8,128)(2,1)S(1)} collective-permute-done((bf16[32,2688]{1,0:T(8,128)(2,1)S(1)}, bf16[32,2688]{1,0:T(8,128)(2,1)S(1)}, u32[]{:S(2)}, u32[]{:S(2)}) %collective-permute-start.25) | collective-permute-done | bytes 172064 | tf_op jit(solution)/shard_map/ppermute | solution.py:121
  127.2 2.1 constant_dynamic-update-slice_fusion.5
  129.3 4.5 %fusion.90 = bf16[256,928]{0,1:T(8,128)(2,1)S(1)} fusion(bf16[256,2688]{1,0:T(8,128)(2,1)} %constant_dynamic-update-slice_fusion.5, bf16[1,2688,928]{1,2,0:T(8,128)(2,1)} %param.37), kind=kOutput, calls=%fused_computation.88 | convolution fusion | flops 1277878272 | bytes 6840320 | tf_op jit(solution)/shard_map/dot_general | solution.py:127
  133.8 1.7 fusion.19
  139.7 2.7 %collective-permute-done.30 = bf16[32,2688]{1,0:T(8,128)(2,1)S(1)} collective-permute-done((bf16[32,2688]{1,0:T(8,128)(2,1)S(1)}, bf16[32,2688]{1,0:T(8,128)(2,1)S(1)}, u32[]{:S(2)}, u32[]{:S(2)}) %collective-permute-start.30) | collective-permute-done | bytes 172064 | tf_op jit(solution)/shard_map/ppermute | solution.py:121
  142.5 4.5 %collective-permute-done.29 = bf16[32,2688]{1,0:T(8,128)(2,1)S(1)} collective-permute-done((bf16[32,2688]{1,0:T(8,128)(2,1)S(1)}, bf16[32,2688]{1,0:T(8,128)(2,1)S(1)}, u32[]{:S(2)}, u32[]{:S(2)}) %collective-permute-start.29) | collective-permute-done | bytes 172064 | tf_op jit(solution)/shard_map/ppermute | solution.py:121
  148.3 6.4 %collective-permute-done.27 = bf16[64,2816]{1,0:T(8,128)(2,1)S(1)} collective-permute-done((bf16[64,2816]{1,0:T(8,128)(2,1)S(1)}, bf16[64,2816]{1,0:T(8,128)(2,1)S(1)}, u32[]{:S(2)}, u32[]{:S(2)}) %collective-permute-start.27) | collective-permute-done | bytes 360480 | tf_op jit(solution)/shard_map/ppermute | solution.py:121
  160.0 4.1 %fusion.87 = bf16[256,928]{0,1:T(8,128)(2,1)S(1)} fusion(bf16[256,2688]{1,0:T(8,128)(2,1)S(1)} %constant_dynamic-update-slice_fusion.10, bf16[1,2688,928]{1,2,0:T(8,128)(2,1)} %param.37), kind=kOutput, calls=%fused_computation.87 | convolution fusion | flops 1277878272 | bytes 6840320 | tf_op jit(solution)/shard_map/dot_general | solution.py:127
  164.2 1.7 fusion.22
  174.8 2.7 %collective-permute-done.41 = bf16[32,2688]{1,0:T(8,128)(2,1)S(1)} collective-permute-done((bf16[32,2688]{1,0:T(8,128)(2,1)S(1)}, bf16[32,2688]{1,0:T(8,128)(2,1)S(1)}, u32[]{:S(2)}, u32[]{:S(2)}) %collective-permute-start.41) | collective-permute-done | bytes 172064 | tf_op jit(solution)/shard_map/ppermute | solution.py:121
  177.5 10.0 %collective-permute-done.33 = bf16[64,2816]{1,0:T(8,128)(2,1)S(1)} collective-permute-done((bf16[64,2816]{1,0:T(8,128)(2,1)S(1)}, bf16[64,2816]{1,0:T(8,128)(2,1)S(1)}, u32[]{:S(2)}, u32[]{:S(2)}) %collective-permute-start.33) | collective-permute-done | bytes 360480 | tf_op jit(solution)/shard_map/ppermute | solution.py:121
  188.9 1.8 collective-permute-start.45
  193.9 4.1 %fusion.84 = bf16[256,928]{0,1:T(8,128)(2,1)S(1)} fusion(bf16[256,2688]{1,0:T(8,128)(2,1)S(1)} %constant_dynamic-update-slice_fusion.15, bf16[1,2688,928]{1,2,0:T(8,128)(2,1)} %param.37), kind=kOutput, calls=%fused_computation.86 | convolution fusion | flops 1277878272 | bytes 6840320 | tf_op jit(solution)/shard_map/dot_general | solution.py:127
  198.1 1.7 fusion.25
  204.5 2.3 collective-permute-done.47
  206.8 4.8 %collective-permute-done.48 = bf16[32,2688]{1,0:T(8,128)(2,1)S(1)} collective-permute-done((bf16[32,2688]{1,0:T(8,128)(2,1)S(1)}, bf16[32,2688]{1,0:T(8,128)(2,1)S(1)}, u32[]{:S(2)}, u32[]{:S(2)}) %collective-permute-start.48) | collective-permute-done | bytes 172064 | tf_op jit(solution)/shard_map/ppermute | solution.py:121
  213.4 1.7 collective-permute-done.55
  216.7 1.7 fusion.28
  222.8 2.0 collective-permute-done.51
  226.8 2.3 collective-permute-done.53
  229.4 3.0 %collective-permute-start.54 = (bf16[64,2688]{1,0:T(8,128)(2,1)S(1)}, bf16[64,2688]{1,0:T(8,128)(2,1)S(1)}, u32[]{:S(2)}, u32[]{:S(2)}) collective-permute-start(bf16[64,2688]{1,0:T(8,128)(2,1)S(1)} %convolution_convert_fusion.1), channel_id=1, source_target_pairs={{0,16},{1,17},{2,18},{3,19},{4,20},{5,21},{6,22},{7,23},{8,24},{9,... | collective-permute-start | bytes 1032200 | tf_op jit(solution)/shard_map/ppermute | solution.py:121
  232.4 1.7 collective-permute-done.58
  234.1 2.3 collective-permute-done.59
  238.3 16.1 %collective-permute-done.54 = bf16[64,2688]{1,0:T(8,128)(2,1)S(1)} collective-permute-done((bf16[64,2688]{1,0:T(8,128)(2,1)S(1)}, bf16[64,2688]{1,0:T(8,128)(2,1)S(1)}, u32[]{:S(2)}, u32[]{:S(2)}) %collective-permute-start.54) | collective-permute-done | bytes 344096 | tf_op jit(solution)/shard_map/ppermute | solution.py:121
  254.4 8.7 %collective-permute-done.60 = bf16[64,2688]{1,0:T(8,128)(2,1)S(1)} collective-permute-done((bf16[64,2688]{1,0:T(8,128)(2,1)S(1)}, bf16[64,2688]{1,0:T(8,128)(2,1)S(1)}, u32[]{:S(2)}, u32[]{:S(2)}) %collective-permute-start.60) | collective-permute-done | bytes 344096 | tf_op jit(solution)/shard_map/ppermute | solution.py:121
  (383 shorter events, 81.6 us)
Async XLA Ops:
  1.1 31.1 %collective-permute-start = (bf16[176,1024]{1,0:T(8,128)(2,1)S(1)}, bf16[176,1024]{1,0:T(8,128)(2,1)}, u32[]{:S(2)}, u32[]{:S(2)}) collective-permute-start(bf16[176,1024]{1,0:T(8,128)(2,1)S(1)} %slice.444), channel_id=1, source_target_pairs={{0,8},{8,16},{16,24},{24,28},{28,20},{20,12},{12,4},{4,0},{1,9},{9... | collective-permute-start | bytes 1081352 | tf_op jit(solution)/shard_map/ppermute | solution.py:25
  2.4 29.8 %collective-permute-start.2 = (bf16[176,1024]{1,0:T(8,128)(2,1)S(1)}, bf16[176,1024]{1,0:T(8,128)(2,1)}, u32[]{:S(2)}, u32[]{:S(2)}) collective-permute-start(bf16[176,1024]{1,0:T(8,128)(2,1)S(1)} %slice.444), channel_id=1, source_target_pairs={{0,4},{8,0},{16,8},{24,16},{28,24},{20,28},{12,20},{4,12},{1,5},{9... | collective-permute-start | bytes 1081352 | tf_op jit(solution)/shard_map/ppermute | solution.py:25
  3.6 28.6 %collective-permute-start.1 = (bf16[160,1024]{1,0:T(8,128)(2,1)S(1)}, bf16[160,1024]{1,0:T(8,128)(2,1)}, u32[]{:S(2)}, u32[]{:S(2)}) collective-permute-start(bf16[160,1024]{1,0:T(8,128)(2,1)S(1)} %slice.445), channel_id=1, source_target_pairs={{0,8},{8,16},{16,24},{24,28},{28,20},{20,12},{12,4},{4,0},{1,9},{9... | collective-permute-start | bytes 983048 | tf_op jit(solution)/shard_map/ppermute | solution.py:25
  5.0 27.2 %collective-permute-start.3 = (bf16[160,1024]{1,0:T(8,128)(2,1)S(1)}, bf16[160,1024]{1,0:T(8,128)(2,1)}, u32[]{:S(2)}, u32[]{:S(2)}) collective-permute-start(bf16[160,1024]{1,0:T(8,128)(2,1)S(1)} %slice.445), channel_id=1, source_target_pairs={{0,4},{8,0},{16,8},{24,16},{28,24},{20,28},{12,20},{4,12},{1,5},{9... | collective-permute-start | bytes 983048 | tf_op jit(solution)/shard_map/ppermute | solution.py:25
  7.6 24.6 %collective-permute-start.4 = (bf16[528,128]{1,0:T(8,128)(2,1)S(1)}, bf16[528,128]{1,0:T(8,128)(2,1)S(1)}, u32[]{:S(2)}, u32[]{:S(2)}) collective-permute-start(bf16[528,128]{1,0:T(8,128)(2,1)S(1)} %pad_maximum_fusion.5), channel_id=1, source_target_pairs={{0,4},{4,0},{8,12},{12,8},{16,20},{20,16},{24,28},{28,24},{1,5},{5... | collective-permute-start | bytes 405512 | tf_op jit(solution)/shard_map/ppermute | solution.py:52
  32.7 9.1 %collective-permute-start.5 = (bf16[528,128]{1,0:T(8,128)(2,1)S(1)}, bf16[528,128]{1,0:T(8,128)(2,1)S(1)}, u32[]{:S(2)}, u32[]{:S(2)}) collective-permute-start(bf16[528,128]{1,0:T(8,128)(2,1)S(1)} %pad_maximum_fusion.6), channel_id=1, source_target_pairs={{0,8},{4,12},{8,16},{12,20},{16,24},{20,28},{1,9},{5,13},{9,17},{1... | collective-permute-start | bytes 405512 | tf_op jit(solution)/shard_map/ppermute | solution.py:75
  35.9 9.0 %collective-permute-start.6 = (bf16[528,128]{1,0:T(8,128)(2,1)S(1)}, bf16[528,128]{1,0:T(8,128)(2,1)S(1)}, u32[]{:S(2)}, u32[]{:S(2)}) collective-permute-start(bf16[528,128]{1,0:T(8,128)(2,1)S(1)} %pad_maximum_fusion.6), channel_id=1, source_target_pairs={{0,16},{4,20},{8,24},{12,28},{1,17},{5,21},{9,25},{13,29},{2,18},{... | collective-permute-start | bytes 405512 | tf_op jit(solution)/shard_map/ppermute | solution.py:75
  38.3 6.8 %collective-permute-start.7 = (bf16[528,128]{1,0:T(8,128)(2,1)S(1)}, bf16[528,128]{1,0:T(8,128)(2,1)S(1)}, u32[]{:S(2)}, u32[]{:S(2)}) collective-permute-start(bf16[528,128]{1,0:T(8,128)(2,1)S(1)} %pad_maximum_fusion.6), channel_id=1, source_target_pairs={{0,24},{4,28},{1,25},{5,29},{2,26},{6,30},{3,27},{7,31}} | collective-permute-start | bytes 405512 | tf_op jit(solution)/shard_map/ppermute | solution.py:75
  39.1 29.6 %collective-permute-start.11 = (bf16[176,1024]{1,0:T(8,128)(2,1)}, bf16[176,1024]{1,0:T(8,128)(2,1)}, u32[]{:S(2)}, u32[]{:S(2)}) collective-permute-start(bf16[176,1024]{1,0:T(8,128)(2,1)} %collective-permute-done.2), channel_id=1, source_target_pairs={{0,4},{8,0},{16,8},{24,16},{28,24},{20,28},{12,20},{4,12},{1,5},{9... | collective-permute-start | bytes 1081352 | tf_op jit(solution)/shard_map/ppermute | solution.py:25
  41.8 26.8 %collective-permute-start.9 = (bf16[176,1024]{1,0:T(8,128)(2,1)}, bf16[176,1024]{1,0:T(8,128)(2,1)}, u32[]{:S(2)}, u32[]{:S(2)}) collective-permute-start(bf16[176,1024]{1,0:T(8,128)(2,1)} %collective-permute-done), channel_id=1, source_target_pairs={{0,8},{8,16},{16,24},{24,28},{28,20},{20,12},{12,4},{4,0},{1,9},{9... | collective-permute-start | bytes 1081352 | tf_op jit(solution)/shard_map/ppermute | solution.py:25
  41.8 20.3 %collective-permute-start.10 = (bf16[160,1024]{1,0:T(8,128)(2,1)}, bf16[160,1024]{1,0:T(8,128)(2,1)}, u32[]{:S(2)}, u32[]{:S(2)}) collective-permute-start(bf16[160,1024]{1,0:T(8,128)(2,1)} %collective-permute-done.1), channel_id=1, source_target_pairs={{0,8},{8,16},{16,24},{24,28},{28,20},{20,12},{12,4},{4,0},{1,9},{9... | collective-permute-start | bytes 983048 | tf_op jit(solution)/shard_map/ppermute | solution.py:25
  44.9 19.4 %collective-permute-start.12 = (bf16[160,1024]{1,0:T(8,128)(2,1)}, bf16[160,1024]{1,0:T(8,128)(2,1)}, u32[]{:S(2)}, u32[]{:S(2)}) collective-permute-start(bf16[160,1024]{1,0:T(8,128)(2,1)} %collective-permute-done.3), channel_id=1, source_target_pairs={{0,4},{8,0},{16,8},{24,16},{28,24},{20,28},{12,20},{4,12},{1,5},{9... | collective-permute-start | bytes 983048 | tf_op jit(solution)/shard_map/ppermute | solution.py:25
  62.1 18.9 %collective-permute-start.16 = (bf16[160,1024]{1,0:T(8,128)(2,1)}, bf16[160,1024]{1,0:T(8,128)(2,1)}, u32[]{:S(2)}, u32[]{:S(2)}) collective-permute-start(bf16[160,1024]{1,0:T(8,128)(2,1)} %collective-permute-done.10), channel_id=1, source_target_pairs={{0,8},{8,16},{16,24},{24,28},{28,20},{20,12},{12,4},{4,0},{1,9},{9... | collective-permute-start | bytes 983048 | tf_op jit(solution)/shard_map/ppermute | solution.py:25
  64.3 12.8 %collective-permute-start.18 = (bf16[160,1024]{1,0:T(8,128)(2,1)}, bf16[160,1024]{1,0:T(8,128)(2,1)}, u32[]{:S(2)}, u32[]{:S(2)}) collective-permute-start(bf16[160,1024]{1,0:T(8,128)(2,1)} %collective-permute-done.12), channel_id=1, source_target_pairs={{0,4},{8,0},{16,8},{24,16},{28,24},{20,28},{12,20},{4,12},{1,5},{9... | collective-permute-start | bytes 983048 | tf_op jit(solution)/shard_map/ppermute | solution.py:25
  68.6 12.4 %collective-permute-start.15 = (bf16[176,1024]{1,0:T(8,128)(2,1)}, bf16[176,1024]{1,0:T(8,128)(2,1)}, u32[]{:S(2)}, u32[]{:S(2)}) collective-permute-start(bf16[176,1024]{1,0:T(8,128)(2,1)} %collective-permute-done.9), channel_id=1, source_target_pairs={{0,8},{8,16},{16,24},{24,28},{28,20},{20,12},{12,4},{4,0},{1,9},{9... | collective-permute-start | bytes 1081352 | tf_op jit(solution)/shard_map/ppermute | solution.py:25
  70.5 10.5 %collective-permute-start.17 = (bf16[176,1024]{1,0:T(8,128)(2,1)}, bf16[176,1024]{1,0:T(8,128)(2,1)}, u32[]{:S(2)}, u32[]{:S(2)}) collective-permute-start(bf16[176,1024]{1,0:T(8,128)(2,1)} %collective-permute-done.11), channel_id=1, source_target_pairs={{0,4},{8,0},{16,8},{24,16},{28,24},{20,28},{12,20},{4,12},{1,5},{9... | collective-permute-start | bytes 1081352 | tf_op jit(solution)/shard_map/ppermute | solution.py:25
  72.5 23.3 %collective-permute-start.13 = (bf16[2,5,64,336]{3,2,0,1:T(8,128)(2,1)S(1)}, bf16[2,5,64,336]{3,2,0,1:T(8,128)(2,1)S(1)}, u32[]{:S(2)}, u32[]{:S(2)}) collective-permute-start(bf16[2,5,64,336]{3,2,0,1:T(8,128)(2,1)S(1)} %dynamic-slice_bitcast_fusion), channel_id=1, source_target_pairs={{0,1},{1,0},{2,3},{3,2},{4,5},{5,4},{6,7},{7,6},{8,9},{9,8},{10,11... | collective-permute-start | bytes 1290248 | tf_op jit(solution)/shard_map/ppermute | solution.py:113
  77.1 10.4 %collective-permute-start.20 = (bf16[160,1024]{1,0:T(8,128)(2,1)}, bf16[160,1024]{1,0:T(8,128)(2,1)}, u32[]{:S(2)}, u32[]{:S(2)}) collective-permute-start(bf16[160,1024]{1,0:T(8,128)(2,1)} %collective-permute-done.18), channel_id=1, source_target_pairs={{0,4},{8,0},{16,8},{24,16},{28,24},{20,28},{12,20},{4,12},{1,5},{9... | collective-permute-start | bytes 983048 | tf_op jit(solution)/shard_map/ppermute | solution.py:25
  81.0 7.7 %collective-permute-start.19 = (bf16[176,1024]{1,0:T(8,128)(2,1)}, bf16[176,1024]{1,0:T(8,128)(2,1)}, u32[]{:S(2)}, u32[]{:S(2)}) collective-permute-start(bf16[176,1024]{1,0:T(8,128)(2,1)} %collective-permute-done.15), channel_id=1, source_target_pairs={{0,8},{8,16},{16,24},{24,28},{28,20},{20,12},{12,4},{4,0},{1,9},{9... | collective-permute-start | bytes 1081352 | tf_op jit(solution)/shard_map/ppermute | solution.py:25
  90.6 6.6 %collective-permute-start.21 = (bf16[2,3,64,336]{3,2,1,0:T(8,128)(2,1)S(1)}, bf16[2,3,64,336]{3,2,1,0:T(8,128)(2,1)S(1)}, u32[]{:S(2)}, u32[]{:S(2)}) collective-permute-start(bf16[2,3,64,336]{3,2,1,0:T(8,128)(2,1)S(1)} %bitcast.281), channel_id=1, source_target_pairs={{0,1},{1,0},{2,3},{3,2},{4,5},{5,4},{6,7},{7,6},{8,9},{9,8},{10,11... | collective-permute-start | bytes 774152 | tf_op jit(solution)/shard_map/ppermute | solution.py:113
  96.0 7.6 %collective-permute-start.14 = (bf16[1,5,64,336]{3,2,0,1:T(8,128)(2,1)S(1)}, bf16[1,5,64,336]{3,2,0,1:T(8,128)(2,1)S(1)}, u32[]{:S(2)}, u32[]{:S(2)}) collective-permute-start(bf16[1,5,64,336]{3,2,0,1:T(8,128)(2,1)S(1)} %constant_dynamic-slice_fusion.4), channel_id=1, source_target_pairs={{0,2},{1,3},{2,0},{3,1},{4,6},{5,7},{6,4},{7,5},{8,10},{9,11},{10,... | collective-permute-start | bytes 645128 | tf_op jit(solution)/shard_map/ppermute | solution.py:113
  97.4 9.3 %collective-permute-start.22 = (bf16[1,3,64,336]{3,2,1,0:T(8,128)(2,1)S(1)}, bf16[1,3,64,336]{3,2,1,0:T(8,128)(2,1)S(1)}, u32[]{:S(2)}, u32[]{:S(2)}) collective-permute-start(bf16[1,3,64,336]{3,2,1,0:T(8,128)(2,1)S(1)} %constant_dynamic-slice_fusion.1), channel_id=1, source_target_pairs={{0,2},{1,3},{2,0},{3,1},{4,6},{5,7},{6,4},{7,5},{8,10},{9,11},{10,... | collective-permute-start | bytes 387080 | tf_op jit(solution)/shard_map/ppermute | solution.py:113
  109.9 13.1 %collective-permute-start.23 = (bf16[64,2816]{1,0:T(8,128)(2,1)S(1)}, bf16[64,2816]{1,0:T(8,128)(2,1)S(1)}, u32[]{:S(2)}, u32[]{:S(2)}) collective-permute-start(bf16[64,2816]{1,0:T(8,128)(2,1)S(1)} %fusion.145), channel_id=1, source_target_pairs={{0,8},{1,9},{2,10},{3,11},{4,12},{5,13},{6,14},{7,15},{8,0},{9,1},... | collective-permute-start | bytes 1081352 | tf_op jit(solution)/shard_map/ppermute | solution.py:121
  113.0 9.9 %collective-permute-start.25 = (bf16[32,2688]{1,0:T(8,128)(2,1)S(1)}, bf16[32,2688]{1,0:T(8,128)(2,1)S(1)}, u32[]{:S(2)}, u32[]{:S(2)}) collective-permute-start(bf16[32,2688]{1,0:T(8,128)(2,1)S(1)} %convolution_convert_fusion.16), channel_id=1, source_target_pairs={{0,4},{1,5},{2,6},{3,7},{4,0},{5,1},{6,2},{7,3},{8,12},{9,13},{10,... | collective-permute-start | bytes 516104 | tf_op jit(solution)/shard_map/ppermute | solution.py:121
  114.5 8.5 %collective-permute-start.24 = (bf16[32,2688]{1,0:T(8,128)(2,1)S(1)}, bf16[32,2688]{1,0:T(8,128)(2,1)S(1)}, u32[]{:S(2)}, u32[]{:S(2)}) collective-permute-start(bf16[32,2688]{1,0:T(8,128)(2,1)S(1)} %convolution_convert_fusion.17), channel_id=1, source_target_pairs={{0,2},{1,3},{2,0},{3,1},{4,6},{5,7},{6,4},{7,5},{8,10},{9,11},{10,... | collective-permute-start | bytes 516104 | tf_op jit(solution)/shard_map/ppermute | solution.py:121
  136.0 6.4 %collective-permute-start.30 = (bf16[32,2688]{1,0:T(8,128)(2,1)S(1)}, bf16[32,2688]{1,0:T(8,128)(2,1)S(1)}, u32[]{:S(2)}, u32[]{:S(2)}) collective-permute-start(bf16[32,2688]{1,0:T(8,128)(2,1)S(1)} %convolution_convert_fusion.11), channel_id=1, source_target_pairs={{0,6},{1,7},{2,4},{3,5},{4,2},{5,3},{6,0},{7,1},{8,14},{9,15},{10,... | collective-permute-start | bytes 516104 | tf_op jit(solution)/shard_map/ppermute | solution.py:121
  137.3 9.6 %collective-permute-start.29 = (bf16[32,2688]{1,0:T(8,128)(2,1)S(1)}, bf16[32,2688]{1,0:T(8,128)(2,1)S(1)}, u32[]{:S(2)}, u32[]{:S(2)}) collective-permute-start(bf16[32,2688]{1,0:T(8,128)(2,1)S(1)} %convolution_convert_fusion.12), channel_id=1, source_target_pairs={{0,4},{1,5},{2,6},{3,7},{4,0},{5,1},{6,2},{7,3},{8,12},{9,13},{10,... | collective-permute-start | bytes 516104 | tf_op jit(solution)/shard_map/ppermute | solution.py:121
  138.0 9.0 %collective-permute-start.28 = (bf16[32,2688]{1,0:T(8,128)(2,1)S(1)}, bf16[32,2688]{1,0:T(8,128)(2,1)S(1)}, u32[]{:S(2)}, u32[]{:S(2)}) collective-permute-start(bf16[32,2688]{1,0:T(8,128)(2,1)S(1)} %convolution_convert_fusion.13), channel_id=1, source_target_pairs={{0,2},{1,3},{2,0},{3,1},{4,6},{5,7},{6,4},{7,5},{8,10},{9,11},{10,... | collective-permute-start | bytes 516104 | tf_op jit(solution)/shard_map/ppermute | solution.py:121
  139.1 15.6 %collective-permute-start.27 = (bf16[64,2816]{1,0:T(8,128)(2,1)S(1)}, bf16[64,2816]{1,0:T(8,128)(2,1)S(1)}, u32[]{:S(2)}, u32[]{:S(2)}) collective-permute-start(bf16[64,2816]{1,0:T(8,128)(2,1)S(1)} %copy-done.22), channel_id=1, source_target_pairs={{0,16},{1,17},{2,18},{3,19},{4,20},{5,21},{6,22},{7,23},{8,24},{9,... | collective-permute-start | bytes 1081352 | tf_op jit(solution)/shard_map/ppermute | solution.py:121
  157.1 11.5 %collective-permute-start.36 = (bf16[32,2688]{1,0:T(8,128)(2,1)S(1)}, bf16[32,2688]{1,0:T(8,128)(2,1)S(1)}, u32[]{:S(2)}, u32[]{:S(2)}) collective-permute-start(bf16[32,2688]{1,0:T(8,128)(2,1)S(1)} %convolution_convert_fusion.7), channel_id=1, source_target_pairs={{0,6},{1,7},{2,4},{3,5},{4,2},{5,3},{6,0},{7,1},{8,14},{9,15},{10,... | collective-permute-start | bytes 516104 | tf_op jit(solution)/shard_map/ppermute | solution.py:121
  158.4 11.1 %collective-permute-start.35 = (bf16[32,2688]{1,0:T(8,128)(2,1)S(1)}, bf16[32,2688]{1,0:T(8,128)(2,1)S(1)}, u32[]{:S(2)}, u32[]{:S(2)}) collective-permute-start(bf16[32,2688]{1,0:T(8,128)(2,1)S(1)} %convolution_convert_fusion.8), channel_id=1, source_target_pairs={{0,4},{1,5},{2,6},{3,7},{4,0},{5,1},{6,2},{7,3},{8,12},{9,13},{10,... | collective-permute-start | bytes 516104 | tf_op jit(solution)/shard_map/ppermute | solution.py:121
  159.0 13.3 %collective-permute-start.34 = (bf16[32,2688]{1,0:T(8,128)(2,1)S(1)}, bf16[32,2688]{1,0:T(8,128)(2,1)S(1)}, u32[]{:S(2)}, u32[]{:S(2)}) collective-permute-start(bf16[32,2688]{1,0:T(8,128)(2,1)S(1)} %convolution_convert_fusion.9), channel_id=1, source_target_pairs={{0,2},{1,3},{2,0},{3,1},{4,6},{5,7},{6,4},{7,5},{8,10},{9,11},{10,... | collective-permute-start | bytes 516104 | tf_op jit(solution)/shard_map/ppermute | solution.py:121
  168.6 6.2 %collective-permute-start.40 = (bf16[32,2688]{1,0:T(8,128)(2,1)S(1)}, bf16[32,2688]{1,0:T(8,128)(2,1)S(1)}, u32[]{:S(2)}, u32[]{:S(2)}) collective-permute-start(bf16[32,2688]{1,0:T(8,128)(2,1)S(1)} %get-tuple-element.234), channel_id=1, source_target_pairs={{0,4},{1,5},{2,6},{3,7},{4,0},{5,1},{6,2},{7,3},{8,12},{9,13},{10,... | collective-permute-start | bytes 516104 | tf_op jit(solution)/shard_map/ppermute | solution.py:121
  169.6 8.0 %collective-permute-start.41 = (bf16[32,2688]{1,0:T(8,128)(2,1)S(1)}, bf16[32,2688]{1,0:T(8,128)(2,1)S(1)}, u32[]{:S(2)}, u32[]{:S(2)}) collective-permute-start(bf16[32,2688]{1,0:T(8,128)(2,1)S(1)} %get-tuple-element.233), channel_id=1, source_target_pairs={{0,6},{1,7},{2,4},{3,5},{4,2},{5,3},{6,0},{7,1},{8,14},{9,15},{10,... | collective-permute-start | bytes 516104 | tf_op jit(solution)/shard_map/ppermute | solution.py:121
  170.7 16.8 %collective-permute-start.33 = (bf16[64,2816]{1,0:T(8,128)(2,1)S(1)}, bf16[64,2816]{1,0:T(8,128)(2,1)S(1)}, u32[]{:S(2)}, u32[]{:S(2)}) collective-permute-start(bf16[64,2816]{1,0:T(8,128)(2,1)S(1)} %copy-done.23), channel_id=1, source_target_pairs={{0,24},{1,25},{2,26},{3,27},{4,28},{5,29},{6,30},{7,31},{8,16},{9,... | collective-permute-start | bytes 1081352 | tf_op jit(solution)/shard_map/ppermute | solution.py:121
  191.0 11.2 %collective-permute-start.44 = (bf16[32,2688]{1,0:T(8,128)(2,1)S(1)}, bf16[32,2688]{1,0:T(8,128)(2,1)S(1)}, u32[]{:S(2)}, u32[]{:S(2)}) collective-permute-start(bf16[32,2688]{1,0:T(8,128)(2,1)S(1)} %convolution_convert_fusion.3), channel_id=1, source_target_pairs={{0,6},{1,7},{2,4},{3,5},{4,2},{5,3},{6,0},{7,1},{8,14},{9,15},{10,... | collective-permute-start | bytes 516104 | tf_op jit(solution)/shard_map/ppermute | solution.py:121
  192.3 12.2 %collective-permute-start.43 = (bf16[32,2688]{1,0:T(8,128)(2,1)S(1)}, bf16[32,2688]{1,0:T(8,128)(2,1)S(1)}, u32[]{:S(2)}, u32[]{:S(2)}) collective-permute-start(bf16[32,2688]{1,0:T(8,128)(2,1)S(1)} %convolution_convert_fusion.4), channel_id=1, source_target_pairs={{0,4},{1,5},{2,6},{3,7},{4,0},{5,1},{6,2},{7,3},{8,12},{9,13},{10,... | collective-permute-start | bytes 516104 | tf_op jit(solution)/shard_map/ppermute | solution.py:121
  192.9 11.6 %collective-permute-start.42 = (bf16[32,2688]{1,0:T(8,128)(2,1)S(1)}, bf16[32,2688]{1,0:T(8,128)(2,1)S(1)}, u32[]{:S(2)}, u32[]{:S(2)}) collective-permute-start(bf16[32,2688]{1,0:T(8,128)(2,1)S(1)} %convolution_convert_fusion.5), channel_id=1, source_target_pairs={{0,2},{1,3},{2,0},{3,1},{4,6},{5,7},{6,4},{7,5},{8,10},{9,11},{10,... | collective-permute-start | bytes 516104 | tf_op jit(solution)/shard_map/ppermute | solution.py:121
  200.9 6.0 %collective-permute-start.47 = (bf16[32,2688]{1,0:T(8,128)(2,1)S(1)}, bf16[32,2688]{1,0:T(8,128)(2,1)S(1)}, u32[]{:S(2)}, u32[]{:S(2)}) collective-permute-start(bf16[32,2688]{1,0:T(8,128)(2,1)S(1)} %get-tuple-element.231), channel_id=1, source_target_pairs={{0,2},{1,3},{2,0},{3,1},{4,6},{5,7},{6,4},{7,5},{8,10},{9,11},{10,... | collective-permute-start | bytes 516104 | tf_op jit(solution)/shard_map/ppermute | solution.py:121
  202.3 9.4 %collective-permute-start.48 = (bf16[32,2688]{1,0:T(8,128)(2,1)S(1)}, bf16[32,2688]{1,0:T(8,128)(2,1)S(1)}, u32[]{:S(2)}, u32[]{:S(2)}) collective-permute-start(bf16[32,2688]{1,0:T(8,128)(2,1)S(1)} %get-tuple-element.230), channel_id=1, source_target_pairs={{0,4},{1,5},{2,6},{3,7},{4,0},{5,1},{6,2},{7,3},{8,12},{9,13},{10,... | collective-permute-start | bytes 516104 | tf_op jit(solution)/shard_map/ppermute | solution.py:121
  203.2 8.4 %collective-permute-start.49 = (bf16[32,2688]{1,0:T(8,128)(2,1)S(1)}, bf16[32,2688]{1,0:T(8,128)(2,1)S(1)}, u32[]{:S(2)}, u32[]{:S(2)}) collective-permute-start(bf16[32,2688]{1,0:T(8,128)(2,1)S(1)} %get-tuple-element.229), channel_id=1, source_target_pairs={{0,6},{1,7},{2,4},{3,5},{4,2},{5,3},{6,0},{7,1},{8,14},{9,15},{10,... | collective-permute-start | bytes 516104 | tf_op jit(solution)/shard_map/ppermute | solution.py:121
  211.9 26.4 %collective-permute-start.50 = (bf16[64,2688]{1,0:T(8,128)(2,1)S(1)}, bf16[64,2688]{1,0:T(8,128)(2,1)S(1)}, u32[]{:S(2)}, u32[]{:S(2)}) collective-permute-start(bf16[64,2688]{1,0:T(8,128)(2,1)S(1)} %convolution_convert_fusion.2), channel_id=1, source_target_pairs={{0,8},{1,9},{2,10},{3,11},{4,12},{5,13},{6,14},{7,15},{8,0},{9,1},... | collective-permute-start | bytes 1032200 | tf_op jit(solution)/shard_map/ppermute | solution.py:121
  220.4 8.7 %collective-permute-start.53 = (bf16[32,2688]{1,0:T(8,128)(2,1)S(1)}, bf16[32,2688]{1,0:T(8,128)(2,1)S(1)}, u32[]{:S(2)}, u32[]{:S(2)}) collective-permute-start(bf16[32,2688]{1,0:T(8,128)(2,1)S(1)} %get-tuple-element.222), channel_id=1, source_target_pairs={{0,6},{1,7},{2,4},{3,5},{4,2},{5,3},{6,0},{7,1},{8,14},{9,15},{10,... | collective-permute-start | bytes 516104 | tf_op jit(solution)/shard_map/ppermute | solution.py:121
  221.9 10.5 %collective-permute-start.57 = (bf16[32,2688]{1,0:T(8,128)(2,1)S(1)}, bf16[32,2688]{1,0:T(8,128)(2,1)S(1)}, u32[]{:S(2)}, u32[]{:S(2)}) collective-permute-start(bf16[32,2688]{1,0:T(8,128)(2,1)S(1)} %get-tuple-element.228), channel_id=1, source_target_pairs={{0,2},{1,3},{2,0},{3,1},{4,6},{5,7},{6,4},{7,5},{8,10},{9,11},{10,... | collective-permute-start | bytes 516104 | tf_op jit(solution)/shard_map/ppermute | solution.py:121
  224.9 9.3 %collective-permute-start.58 = (bf16[32,2688]{1,0:T(8,128)(2,1)S(1)}, bf16[32,2688]{1,0:T(8,128)(2,1)S(1)}, u32[]{:S(2)}, u32[]{:S(2)}) collective-permute-start(bf16[32,2688]{1,0:T(8,128)(2,1)S(1)} %get-tuple-element.227), channel_id=1, source_target_pairs={{0,4},{1,5},{2,6},{3,7},{4,0},{5,1},{6,2},{7,3},{8,12},{9,13},{10,... | collective-permute-start | bytes 516104 | tf_op jit(solution)/shard_map/ppermute | solution.py:121
  225.7 10.7 %collective-permute-start.59 = (bf16[32,2688]{1,0:T(8,128)(2,1)S(1)}, bf16[32,2688]{1,0:T(8,128)(2,1)S(1)}, u32[]{:S(2)}, u32[]{:S(2)}) collective-permute-start(bf16[32,2688]{1,0:T(8,128)(2,1)S(1)} %get-tuple-element.226), channel_id=1, source_target_pairs={{0,6},{1,7},{2,4},{3,5},{4,2},{5,3},{6,0},{7,1},{8,14},{9,15},{10,... | collective-permute-start | bytes 516104 | tf_op jit(solution)/shard_map/ppermute | solution.py:121
  229.4 24.9 %collective-permute-start.54 = (bf16[64,2688]{1,0:T(8,128)(2,1)S(1)}, bf16[64,2688]{1,0:T(8,128)(2,1)S(1)}, u32[]{:S(2)}, u32[]{:S(2)}) collective-permute-start(bf16[64,2688]{1,0:T(8,128)(2,1)S(1)} %convolution_convert_fusion.1), channel_id=1, source_target_pairs={{0,16},{1,17},{2,18},{3,19},{4,20},{5,21},{6,22},{7,23},{8,24},{9,... | collective-permute-start | bytes 1032200 | tf_op jit(solution)/shard_map/ppermute | solution.py:121
  236.7 26.3 %collective-permute-start.60 = (bf16[64,2688]{1,0:T(8,128)(2,1)S(1)}, bf16[64,2688]{1,0:T(8,128)(2,1)S(1)}, u32[]{:S(2)}, u32[]{:S(2)}) collective-permute-start(bf16[64,2688]{1,0:T(8,128)(2,1)S(1)} %convolution_convert_fusion), channel_id=1, source_target_pairs={{0,24},{1,25},{2,26},{3,27},{4,28},{5,29},{6,30},{7,31},{8,16},{9,... | collective-permute-start | bytes 1032200 | tf_op jit(solution)/shard_map/ppermute | solution.py:121
  (59 other events, 323.0 us)
where the time goes:
time: 265 us; the launch traced here: 264 us
  waiting for transfers between devices  104 us (39%)
  starting transfers between devices  71.6 us (27%)
  matrix products  38.6 us (15%)
  local copies, waits for them, and re-layouts  23.8 us (9%)
  between operations  16.6 us (6%)
  other arithmetic  9 us (3%)
    ppermute x38, waiting for transfers between devices, across(): lax.ppermute(x, axes, [(i, i ^ mask) for i in range(lax.axis_size(axes))])  78.7 us
    ppermute x38, starting transfers between devices, across(): lax.ppermute(x, axes, [(i, i ^ mask) for i in range(lax.axis_size(axes))])  36.3 us
    ppermute x14, starting transfers between devices, shift(): lax.ppermute(x, axis, [(order[i], order[(i + step) % size]) for i in rang...  15.5 us
    dot_general x4, matrix products, expert_half(): jnp.dot(flat_rows, up_weight[0], preferred_element_type=jnp.float32)  14.2 us
    ppermute x4, starting transfers between devices, head_scatter(): came = lax.ppermute(send, axis, [(i, i ^ stride) for i in range(size)])  12 us
    ppermute x14, waiting for transfers between devices, shift(): lax.ppermute(x, axis, [(order[i], order[(i + step) % size]) for i in rang...  10.7 us
    ppermute x4, waiting for transfers between devices, head_scatter(): came = lax.ppermute(send, axis, [(i, i ^ stride) for i in range(size)])  8.21 us
    dot_general x5, matrix products, product(): lax.dot_general(normed, rows, (((1,), (1,)), ((), ())), preferred_element...  7.62 us
  transfers between devices with their start and end apart: 61, of which 26 were waited for; matrix products, arithmetic and copies ran while one was open for 19% of the time, Pallas kernels for 0%

commit v1 on v0

--- a/solution.py
+++ b/solution.py
@@ -208,7 +208,6 @@
     )
 
     got = swapped(device_decay, device_state, "seq")
-    ring[0], got = lax.optimization_barrier((ring[0], got))
     for step in range(2, seq_size // 2 + 1):
         ring.append(ring_step(ring[-1], "seq", step))
     incoming = entering(got, device_decay, device_state, "seq")
@@ -255,7 +254,7 @@
         ahead, behind = ring[step - 1]
         offsets += [-step, step] if 2 * step < seq_size else [-step]
         products += product([*ahead, *behind])
-        if step in (seq_size // 4, seq_size // 2):
+        if step in (seq_size // 4, seq_size // 2 - 1, seq_size // 2):
             batches.append(head_scatter(jnp.concatenate(products, axis=1), "head"))
             products = []
     scattered = jnp.concatenate(batches, axis=0).astype(jnp.float32)
@@ -352,16 +351,15 @@
     def line(k):
         return across(block, k * stride)
 
-    rows1 = line(1)
+    rows1, rows2 = line(1), line(2)
     sent0 = spread(block)
     rows1, sent0, block = lax.optimization_barrier((rows1, sent0, block))
 
-    rows2 = line(2)
+    rows3 = line(3)
     sent1 = spread(rows1)
     done0 = expert(sent0[0])
-    rows2, sent1, done0, block = lax.optimization_barrier((rows2, sent1, done0, block))
-
-    rows3 = line(3)
+    rows2, sent1, done0 = lax.optimization_barrier((rows2, sent1, done0))
+
     sent2 = spread(rows2)
     done1 = expert(sent1[0])
     back0 = brought(done0)

time: 265 us -> 264 us (level)
  starting transfers between devices: 71.6 us -> 92.7 us
  waiting for transfers between devices: 104 us -> 83.7 us
    ppermute x38, waiting for transfers between devices: 78.7 us -> 67.2 us  [across(): lax.ppermute(x, axes, [(i, i ^ mask) for i in range(lax.axis_size(axes))])]
    ppermute x38, starting transfers between devices: 36.3 us -> 46.3 us  [across(): lax.ppermute(x, axes, [(i, i ^ mask) for i in range(lax.axis_size(axes))])]
    ppermute x4 -> x6, starting transfers between devices: 12 us -> 19.9 us  [head_scatter(): came = lax.ppermute(send, axis, [(i, i ^ stride) for i in range(size)])]
    ppermute x3, starting transfers between devices: 6.18 us -> 13.6 us  [entering(): lax.ppermute(pair, axis, [(i, i + 2 * d) for i in range(size - 2 * d)])]
    ppermute x4 -> x6, waiting for transfers between devices: 8.21 us -> 2.58 us  [head_scatter(): came = lax.ppermute(send, axis, [(i, i ^ stride) for i in range(size)])]
    ppermute x14, waiting for transfers between devices: 10.7 us -> 6.43 us  [shift(): lax.ppermute(x, axis, [(order[i], order[(i + step) % size]) for i in rang...]
    ppermute x14, starting transfers between devices: 15.5 us -> 11.3 us  [shift(): lax.ppermute(x, axis, [(order[i], order[(i + step) % size]) for i in rang...]
    ppermute x3, waiting for transfers between devices: 2.87 us -> 6.88 us  [entering(): lax.ppermute(pair, axis, [(i, i + 2 * d) for i in range(size - 2 * d)])]
  transfers between devices with their start and end apart: 61 -> 63, of which waited for: 26 -> 29; matrix products, arithmetic and copies ran while one was open for 19% -> 21% of each run, Pallas kernels for 0% -> 0%
where the time goes in v1:
time: 264 us; the launch traced here: 263 us
  starting transfers between devices  92.7 us (35%)
  waiting for transfers between devices  83.7 us (32%)
  matrix products  38.1 us (14%)
  local copies, waits for them, and re-layouts  21.3 us (8%)
  between operations  16.4 us (6%)
  other arithmetic  11.1 us (4%)
    ppermute x38, waiting for transfers between devices, across(): lax.ppermute(x, axes, [(i, i ^ mask) for i in range(lax.axis_size(axes))])  67.2 us
    ppermute x38, starting transfers between devices, across(): lax.ppermute(x, axes, [(i, i ^ mask) for i in range(lax.axis_size(axes))])  46.3 us
    ppermute x6, starting transfers between devices, head_scatter(): came = lax.ppermute(send, axis, [(i, i ^ stride) for i in range(size)])  19.9 us
    dot_general x4, matrix products, expert_half(): jnp.dot(flat_rows, up_weight[0], preferred_element_type=jnp.float32)  13.9 us
    ppermute x3, starting transfers between devices, entering(): lax.ppermute(pair, axis, [(i, i + 2 * d) for i in range(size - 2 * d)])  13.6 us
    ppermute x14, starting transfers between devices, shift(): lax.ppermute(x, axis, [(order[i], order[(i + step) % size]) for i in rang...  11.3 us
    dot_general x5, matrix products, product(): lax.dot_general(normed, rows, (((1,), (1,)), ((), ())), preferred_element...  7.29 us
    ppermute x3, waiting for transfers between devices, entering(): lax.ppermute(pair, axis, [(i, i + 2 * d) for i in range(size - 2 * d)])  6.88 us
  transfers between devices with their start and end apart: 63, of which 29 were waited for; matrix products, arithmetic and copies ran while one was open for 21% of the time, Pallas kernels for 0%

profile of v1, /device:TPU:9, one launch (start us, length us, event | category | flops | bytes accessed | tf_op | source)
XLA Modules:
  0.0 263.4 jit_solution(12844241368567822378)
XLA Ops:
  0.0 1.8 slice.456
  3.3 1.7 slice.457
  12.2 1.8 convolution_bitcast_fusion
  34.6 11.0 %collective-permute-start.2 = (bf16[528,128]{1,0:T(8,128)(2,1)S(1)}, bf16[528,128]{1,0:T(8,128)(2,1)S(1)}, u32[]{:S(2)}, u32[]{:S(2)}) collective-permute-start(bf16[528,128]{1,0:T(8,128)(2,1)S(1)} %pad_maximum_fusion.5), channel_id=1, source_target_pairs={{0,16},{4,20},{8,24},{12,28},{1,17},{5,21},{9,25},{13,29},{2,18},{... | collective-permute-start | bytes 405512 | tf_op jit(solution)/shard_map/ppermute | solution.py:75
  45.8 3.2 %collective-permute-done.2 = bf16[528,128]{1,0:T(8,128)(2,1)S(1)} collective-permute-done((bf16[528,128]{1,0:T(8,128)(2,1)S(1)}, bf16[528,128]{1,0:T(8,128)(2,1)S(1)}, u32[]{:S(2)}, u32[]{:S(2)}) %collective-permute-start.2) | collective-permute-done | bytes 135200 | tf_op jit(solution)/shard_map/ppermute | solution.py:75
  49.0 1.9 collective-permute-start.1
  51.1 3.7 %collective-permute-done.1 = bf16[528,128]{1,0:T(8,128)(2,1)S(1)} collective-permute-done((bf16[528,128]{1,0:T(8,128)(2,1)S(1)}, bf16[528,128]{1,0:T(8,128)(2,1)S(1)}, u32[]{:S(2)}, u32[]{:S(2)}) %collective-permute-start.1) | collective-permute-done | bytes 135200 | tf_op jit(solution)/shard_map/ppermute | solution.py:75
  57.2 1.7 collective-permute-start.9
  61.0 1.7 fusion.106
  63.5 1.6 copy.183
  66.5 1.9 fusion.99
  70.6 1.7 collective-permute-start.15
  72.3 1.9 fusion.96
  74.7 9.2 %collective-permute-start.13 = (bf16[2,5,64,336]{3,2,0,1:T(8,128)(2,1)S(1)}, bf16[2,5,64,336]{3,2,0,1:T(8,128)(2,1)S(1)}, u32[]{:S(2)}, u32[]{:S(2)}) collective-permute-start(bf16[2,5,64,336]{3,2,0,1:T(8,128)(2,1)S(1)} %dynamic-slice_bitcast_fusion), channel_id=1, source_target_pairs={{0,1},{1,0},{2,3},{3,2},{4,5},{5,4},{6,7},{7,6},{8,9},{9,8},{10,11... | collective-permute-start | bytes 1290248 | tf_op jit(solution)/shard_map/ppermute | solution.py:113
  84.3 1.8 fusion.93
  86.6 6.6 %collective-permute-start.19 = (bf16[2,2,64,336]{3,2,1,0:T(8,128)(2,1)S(1)}, bf16[2,2,64,336]{3,2,1,0:T(8,128)(2,1)S(1)}, u32[]{:S(2)}, u32[]{:S(2)}) collective-permute-start(bf16[2,2,64,336]{3,2,1,0:T(8,128)(2,1)S(1)} %bitcast.291), channel_id=1, source_target_pairs={{0,1},{1,0},{2,3},{3,2},{4,5},{5,4},{6,7},{7,6},{8,9},{9,8},{10,11... | collective-permute-start | bytes 516104 | tf_op jit(solution)/shard_map/ppermute | solution.py:113
  93.2 1.7 collective-permute-start.21
  96.8 6.4 %collective-permute-done.21 = bf16[176,1024]{1,0:T(8,128)(2,1)S(1)} collective-permute-done((bf16[176,1024]{1,0:T(8,128)(2,1)}, bf16[176,1024]{1,0:T(8,128)(2,1)S(1)}, u32[]{:S(2)}, u32[]{:S(2)}) %collective-permute-start.21) | collective-permute-done | bytes 360480 | tf_op jit(solution)/shard_map/ppermute | solution.py:25
  108.2 1.7 collective-permute-done.24
  113.8 1.8 collective-permute-start.25
  118.9 4.3 %collective-permute-start.30 = (bf16[64,2816]{1,0:T(8,128)(2,1)}, bf16[64,2816]{1,0:T(8,128)(2,1)S(1)}, u32[]{:S(2)}, u32[]{:S(2)}) collective-permute-start(bf16[64,2816]{1,0:T(8,128)(2,1)} %fusion.145), channel_id=1, source_target_pairs={{0,16},{1,17},{2,18},{3,19},{4,20},{5,21},{6,22},{7,23},{8,24},{9,... | collective-permute-start | bytes 1081352 | tf_op jit(solution)/shard_map/ppermute | solution.py:121
  123.4 2.6 collective-permute-done.28
  126.9 2.4 collective-permute-start.34
  131.2 4.1 %fusion.90 = bf16[256,928]{0,1:T(8,128)(2,1)S(1)} fusion(bf16[256,2688]{1,0:T(8,128)(2,1)S(1)} %constant_dynamic-update-slice_fusion.5, bf16[1,2688,928]{1,2,0:T(8,128)(2,1)} %param.37), kind=kOutput, calls=%fused_computation.88 | convolution fusion | flops 1277878272 | bytes 6840320 | tf_op jit(solution)/shard_map/dot_general | solution.py:127
  135.4 1.7 fusion.19
  137.9 4.0 %collective-permute-start.29 = (bf16[64,2816]{1,0:T(8,128)(2,1)}, bf16[64,2816]{1,0:T(8,128)(2,1)S(1)}, u32[]{:S(2)}, u32[]{:S(2)}) collective-permute-start(bf16[64,2816]{1,0:T(8,128)(2,1)} %fusion.145), channel_id=1, source_target_pairs={{0,24},{1,25},{2,26},{3,27},{4,28},{5,29},{6,30},{7,31},{8,16},{9,... | collective-permute-start | bytes 1081352 | tf_op jit(solution)/shard_map/ppermute | solution.py:121
  143.8 1.5 collective-permute-start.33
  145.6 1.8 collective-permute-done.31
  147.5 3.9 %collective-permute-done.33 = bf16[32,2688]{1,0:T(8,128)(2,1)S(1)} collective-permute-done((bf16[32,2688]{1,0:T(8,128)(2,1)S(1)}, bf16[32,2688]{1,0:T(8,128)(2,1)S(1)}, u32[]{:S(2)}, u32[]{:S(2)}) %collective-permute-start.33) | collective-permute-done | bytes 172064 | tf_op jit(solution)/shard_map/ppermute | solution.py:121
  157.1 4.1 %fusion.87 = bf16[256,928]{0,1:T(8,128)(2,1)S(1)} fusion(bf16[256,2688]{1,0:T(8,128)(2,1)S(1)} %constant_dynamic-update-slice_fusion.10, bf16[1,2688,928]{1,2,0:T(8,128)(2,1)} %param.37), kind=kOutput, calls=%fused_computation.87 | convolution fusion | flops 1277878272 | bytes 6840320 | tf_op jit(solution)/shard_map/dot_general | solution.py:127
  161.2 1.7 fusion.22
  172.5 1.7 collective-permute-done.38
  174.2 3.2 %collective-permute-done.41 = bf16[32,2688]{1,0:T(8,128)(2,1)S(1)} collective-permute-done((bf16[32,2688]{1,0:T(8,128)(2,1)S(1)}, bf16[32,2688]{1,0:T(8,128)(2,1)S(1)}, u32[]{:S(2)}, u32[]{:S(2)}) %collective-permute-start.41) | collective-permute-done | bytes 172064 | tf_op jit(solution)/shard_map/ppermute | solution.py:121
  177.4 1.8 collective-permute-done.42
  179.1 2.5 collective-permute-done.43
  188.0 3.4 %collective-permute-start.47 = (bf16[128,2688]{1,0:T(8,128)(2,1)S(1)}, bf16[128,2688]{1,0:T(8,128)(2,1)S(1)}, u32[]{:S(2)}, u32[]{:S(2)}) collective-permute-start(bf16[128,2688]{1,0:T(8,128)(2,1)S(1)} %pad_maximum_fusion.2), channel_id=1, source_target_pairs={{0,1},{1,0},{2,3},{3,2},{4,5},{5,4},{6,7},{7,6},{8,9},{9,8},{10,11... | collective-permute-start | bytes 2064392 | tf_op jit(solution)/shard_map/ppermute | solution.py:121
  193.3 4.1 %fusion.84 = bf16[256,928]{0,1:T(8,128)(2,1)S(1)} fusion(bf16[256,2688]{1,0:T(8,128)(2,1)S(1)} %constant_dynamic-update-slice_fusion.15, bf16[1,2688,928]{1,2,0:T(8,128)(2,1)} %param.37), kind=kOutput, calls=%fused_computation.86 | convolution fusion | flops 1277878272 | bytes 6840320 | tf_op jit(solution)/shard_map/dot_general | solution.py:127
  197.5 1.7 fusion.25
  202.9 2.7 %collective-permute-done.49 = bf16[32,2688]{1,0:T(8,128)(2,1)S(1)} collective-permute-done((bf16[32,2688]{1,0:T(8,128)(2,1)S(1)}, bf16[32,2688]{1,0:T(8,128)(2,1)S(1)}, u32[]{:S(2)}, u32[]{:S(2)}) %collective-permute-start.49) | collective-permute-done | bytes 172064 | tf_op jit(solution)/shard_map/ppermute | solution.py:121
  206.0 3.7 %collective-permute-done.51 = bf16[32,2688]{1,0:T(8,128)(2,1)S(1)} collective-permute-done((bf16[32,2688]{1,0:T(8,128)(2,1)S(1)}, bf16[32,2688]{1,0:T(8,128)(2,1)S(1)}, u32[]{:S(2)}, u32[]{:S(2)}) %collective-permute-start.51) | collective-permute-done | bytes 172064 | tf_op jit(solution)/shard_map/ppermute | solution.py:121
  211.1 1.7 collective-permute-done.57
  212.9 1.6 fusion.81
  214.5 1.7 fusion.28
  219.7 2.0 collective-permute-start.52
  224.4 3.8 %collective-permute-done.54 = bf16[32,2688]{1,0:T(8,128)(2,1)S(1)} collective-permute-done((bf16[32,2688]{1,0:T(8,128)(2,1)S(1)}, bf16[32,2688]{1,0:T(8,128)(2,1)S(1)}, u32[]{:S(2)}, u32[]{:S(2)}) %collective-permute-start.54) | collective-permute-done | bytes 172064 | tf_op jit(solution)/shard_map/ppermute | solution.py:121
  231.0 4.1 %collective-permute-done.60 = bf16[32,2688]{1,0:T(8,128)(2,1)S(1)} collective-permute-done((bf16[32,2688]{1,0:T(8,128)(2,1)S(1)}, bf16[32,2688]{1,0:T(8,128)(2,1)S(1)}, u32[]{:S(2)}, u32[]{:S(2)}) %collective-permute-start.60) | collective-permute-done | bytes 172064 | tf_op jit(solution)/shard_map/ppermute | solution.py:121
  235.5 17.5 %collective-permute-done.56 = bf16[64,2688]{1,0:T(8,128)(2,1)S(1)} collective-permute-done((bf16[64,2688]{1,0:T(8,128)(2,1)S(1)}, bf16[64,2688]{1,0:T(8,128)(2,1)S(1)}, u32[]{:S(2)}, u32[]{:S(2)}) %collective-permute-start.56) | collective-permute-done | bytes 344096 | tf_op jit(solution)/shard_map/ppermute | solution.py:121
  253.0 9.4 %collective-permute-done.62 = bf16[64,2688]{1,0:T(8,128)(2,1)S(1)} collective-permute-done((bf16[64,2688]{1,0:T(8,128)(2,1)S(1)}, bf16[64,2688]{1,0:T(8,128)(2,1)S(1)}, u32[]{:S(2)}, u32[]{:S(2)}) %collective-permute-start.62) | collective-permute-done | bytes 344096 | tf_op jit(solution)/shard_map/ppermute | solution.py:121
  (380 shorter events, 83.5 us)
Async XLA Ops:
  1.8 55.4 %collective-permute-start.5 = (bf16[176,1024]{1,0:T(8,128)(2,1)}, bf16[176,1024]{1,0:T(8,128)(2,1)}, u32[]{:S(2)}, u32[]{:S(2)}) collective-permute-start(bf16[176,1024]{1,0:T(8,128)(2,1)} %slice.456), channel_id=1, source_target_pairs={{0,8},{8,16},{16,24},{24,28},{28,20},{20,12},{12,4},{4,0},{1,9},{9... | collective-permute-start | bytes 1081352 | tf_op jit(solution)/shard_map/ppermute | solution.py:25
  3.1 55.8 %collective-permute-start.7 = (bf16[176,1024]{1,0:T(8,128)(2,1)}, bf16[176,1024]{1,0:T(8,128)(2,1)}, u32[]{:S(2)}, u32[]{:S(2)}) collective-permute-start(bf16[176,1024]{1,0:T(8,128)(2,1)} %slice.456), channel_id=1, source_target_pairs={{0,4},{8,0},{16,8},{24,16},{28,24},{20,28},{12,20},{4,12},{1,5},{9... | collective-permute-start | bytes 1081352 | tf_op jit(solution)/shard_map/ppermute | solution.py:25
  5.0 50.7 %collective-permute-start.8 = (bf16[160,1024]{1,0:T(8,128)(2,1)}, bf16[160,1024]{1,0:T(8,128)(2,1)}, u32[]{:S(2)}, u32[]{:S(2)}) collective-permute-start(bf16[160,1024]{1,0:T(8,128)(2,1)} %slice.457), channel_id=1, source_target_pairs={{0,4},{8,0},{16,8},{24,16},{28,24},{20,28},{12,20},{4,12},{1,5},{9... | collective-permute-start | bytes 983048 | tf_op jit(solution)/shard_map/ppermute | solution.py:25
  5.0 50.7 %collective-permute-start.6 = (bf16[160,1024]{1,0:T(8,128)(2,1)}, bf16[160,1024]{1,0:T(8,128)(2,1)}, u32[]{:S(2)}, u32[]{:S(2)}) collective-permute-start(bf16[160,1024]{1,0:T(8,128)(2,1)} %slice.457), channel_id=1, source_target_pairs={{0,8},{8,16},{16,24},{24,28},{28,20},{20,12},{12,4},{4,0},{1,9},{9... | collective-permute-start | bytes 983048 | tf_op jit(solution)/shard_map/ppermute | solution.py:25
  9.0 24.3 %collective-permute-start = (bf16[528,128]{1,0:T(8,128)(2,1)S(1)}, bf16[528,128]{1,0:T(8,128)(2,1)S(1)}, u32[]{:S(2)}, u32[]{:S(2)}) collective-permute-start(bf16[528,128]{1,0:T(8,128)(2,1)S(1)} %pad_maximum_fusion.4), channel_id=1, source_target_pairs={{0,4},{4,0},{8,12},{12,8},{16,20},{20,16},{24,28},{28,24},{1,5},{5... | collective-permute-start | bytes 405512 | tf_op jit(solution)/shard_map/ppermute | solution.py:52
  34.6 14.4 %collective-permute-start.2 = (bf16[528,128]{1,0:T(8,128)(2,1)S(1)}, bf16[528,128]{1,0:T(8,128)(2,1)S(1)}, u32[]{:S(2)}, u32[]{:S(2)}) collective-permute-start(bf16[528,128]{1,0:T(8,128)(2,1)S(1)} %pad_maximum_fusion.5), channel_id=1, source_target_pairs={{0,16},{4,20},{8,24},{12,28},{1,17},{5,21},{9,25},{13,29},{2,18},{... | collective-permute-start | bytes 405512 | tf_op jit(solution)/shard_map/ppermute | solution.py:75
  55.7 13.4 %collective-permute-start.12 = (bf16[160,1024]{1,0:T(8,128)(2,1)}, bf16[160,1024]{1,0:T(8,128)(2,1)}, u32[]{:S(2)}, u32[]{:S(2)}) collective-permute-start(bf16[160,1024]{1,0:T(8,128)(2,1)} %collective-permute-done.8), channel_id=1, source_target_pairs={{0,4},{8,0},{16,8},{24,16},{28,24},{20,28},{12,20},{4,12},{1,5},{9... | collective-permute-start | bytes 983048 | tf_op jit(solution)/shard_map/ppermute | solution.py:25
  55.8 13.4 %collective-permute-start.10 = (bf16[160,1024]{1,0:T(8,128)(2,1)}, bf16[160,1024]{1,0:T(8,128)(2,1)}, u32[]{:S(2)}, u32[]{:S(2)}) collective-permute-start(bf16[160,1024]{1,0:T(8,128)(2,1)} %collective-permute-done.6), channel_id=1, source_target_pairs={{0,8},{8,16},{16,24},{24,28},{28,20},{20,12},{12,4},{4,0},{1,9},{9... | collective-permute-start | bytes 983048 | tf_op jit(solution)/shard_map/ppermute | solution.py:25
  57.2 13.4 %collective-permute-start.9 = (bf16[176,1024]{1,0:T(8,128)(2,1)}, bf16[176,1024]{1,0:T(8,128)(2,1)}, u32[]{:S(2)}, u32[]{:S(2)}) collective-permute-start(bf16[176,1024]{1,0:T(8,128)(2,1)} %collective-permute-done.5), channel_id=1, source_target_pairs={{0,8},{8,16},{16,24},{24,28},{28,20},{20,12},{12,4},{4,0},{1,9},{9... | collective-permute-start | bytes 1081352 | tf_op jit(solution)/shard_map/ppermute | solution.py:25
  58.9 13.4 %collective-permute-start.11 = (bf16[176,1024]{1,0:T(8,128)(2,1)}, bf16[176,1024]{1,0:T(8,128)(2,1)}, u32[]{:S(2)}, u32[]{:S(2)}) collective-permute-start(bf16[176,1024]{1,0:T(8,128)(2,1)} %collective-permute-done.7), channel_id=1, source_target_pairs={{0,4},{8,0},{16,8},{24,16},{28,24},{20,28},{12,20},{4,12},{1,5},{9... | collective-permute-start | bytes 1081352 | tf_op jit(solution)/shard_map/ppermute | solution.py:25
  69.1 14.9 %collective-permute-start.18 = (bf16[160,1024]{1,0:T(8,128)(2,1)}, bf16[160,1024]{1,0:T(8,128)(2,1)}, u32[]{:S(2)}, u32[]{:S(2)}) collective-permute-start(bf16[160,1024]{1,0:T(8,128)(2,1)} %collective-permute-done.12), channel_id=1, source_target_pairs={{0,4},{8,0},{16,8},{24,16},{28,24},{20,28},{12,20},{4,12},{1,5},{9... | collective-permute-start | bytes 983048 | tf_op jit(solution)/shard_map/ppermute | solution.py:25
  69.2 15.1 %collective-permute-start.16 = (bf16[160,1024]{1,0:T(8,128)(2,1)}, bf16[160,1024]{1,0:T(8,128)(2,1)}, u32[]{:S(2)}, u32[]{:S(2)}) collective-permute-start(bf16[160,1024]{1,0:T(8,128)(2,1)} %collective-permute-done.10), channel_id=1, source_target_pairs={{0,8},{8,16},{16,24},{24,28},{28,20},{20,12},{12,4},{4,0},{1,9},{9... | collective-permute-start | bytes 983048 | tf_op jit(solution)/shard_map/ppermute | solution.py:25
  70.6 13.7 %collective-permute-start.15 = (bf16[176,1024]{1,0:T(8,128)(2,1)}, bf16[176,1024]{1,0:T(8,128)(2,1)}, u32[]{:S(2)}, u32[]{:S(2)}) collective-permute-start(bf16[176,1024]{1,0:T(8,128)(2,1)} %collective-permute-done.9), channel_id=1, source_target_pairs={{0,8},{8,16},{16,24},{24,28},{28,20},{20,12},{12,4},{4,0},{1,9},{9... | collective-permute-start | bytes 1081352 | tf_op jit(solution)/shard_map/ppermute | solution.py:25
  72.3 12.0 %collective-permute-start.17 = (bf16[176,1024]{1,0:T(8,128)(2,1)}, bf16[176,1024]{1,0:T(8,128)(2,1)}, u32[]{:S(2)}, u32[]{:S(2)}) collective-permute-start(bf16[176,1024]{1,0:T(8,128)(2,1)} %collective-permute-done.11), channel_id=1, source_target_pairs={{0,4},{8,0},{16,8},{24,16},{28,24},{20,28},{12,20},{4,12},{1,5},{9... | collective-permute-start | bytes 1081352 | tf_op jit(solution)/shard_map/ppermute | solution.py:25
  74.7 20.2 %collective-permute-start.13 = (bf16[2,5,64,336]{3,2,0,1:T(8,128)(2,1)S(1)}, bf16[2,5,64,336]{3,2,0,1:T(8,128)(2,1)S(1)}, u32[]{:S(2)}, u32[]{:S(2)}) collective-permute-start(bf16[2,5,64,336]{3,2,0,1:T(8,128)(2,1)S(1)} %dynamic-slice_bitcast_fusion), channel_id=1, source_target_pairs={{0,1},{1,0},{2,3},{3,2},{4,5},{5,4},{6,7},{7,6},{8,9},{9,8},{10,11... | collective-permute-start | bytes 1290248 | tf_op jit(solution)/shard_map/ppermute | solution.py:113
  83.9 12.8 %collective-permute-start.22 = (bf16[160,1024]{1,0:T(8,128)(2,1)}, bf16[160,1024]{1,0:T(8,128)(2,1)}, u32[]{:S(2)}, u32[]{:S(2)}) collective-permute-start(bf16[160,1024]{1,0:T(8,128)(2,1)} %collective-permute-done.18), channel_id=1, source_target_pairs={{0,4},{8,0},{16,8},{24,16},{28,24},{20,28},{12,20},{4,12},{1,5},{9... | collective-permute-start | bytes 983048 | tf_op jit(solution)/shard_map/ppermute | solution.py:25
  86.6 9.8 %collective-permute-start.19 = (bf16[2,2,64,336]{3,2,1,0:T(8,128)(2,1)S(1)}, bf16[2,2,64,336]{3,2,1,0:T(8,128)(2,1)S(1)}, u32[]{:S(2)}, u32[]{:S(2)}) collective-permute-start(bf16[2,2,64,336]{3,2,1,0:T(8,128)(2,1)S(1)} %bitcast.291), channel_id=1, source_target_pairs={{0,1},{1,0},{2,3},{3,2},{4,5},{5,4},{6,7},{7,6},{8,9},{9,8},{10,11... | collective-permute-start | bytes 516104 | tf_op jit(solution)/shard_map/ppermute | solution.py:113
  93.2 9.9 %collective-permute-start.21 = (bf16[176,1024]{1,0:T(8,128)(2,1)}, bf16[176,1024]{1,0:T(8,128)(2,1)S(1)}, u32[]{:S(2)}, u32[]{:S(2)}) collective-permute-start(bf16[176,1024]{1,0:T(8,128)(2,1)} %collective-permute-done.15), channel_id=1, source_target_pairs={{0,8},{8,16},{16,24},{24,28},{28,20},{20,12},{12,4},{4,0},{1,9},{9... | collective-permute-start | bytes 1081352 | tf_op jit(solution)/shard_map/ppermute | solution.py:25
  95.1 13.1 %collective-permute-start.14 = (bf16[1,5,64,336]{3,2,0,1:T(8,128)(2,1)S(1)}, bf16[1,5,64,336]{3,2,0,1:T(8,128)(2,1)S(1)}, u32[]{:S(2)}, u32[]{:S(2)}) collective-permute-start(bf16[1,5,64,336]{3,2,0,1:T(8,128)(2,1)S(1)} %constant_dynamic-slice_fusion.3), channel_id=1, source_target_pairs={{0,2},{1,3},{2,0},{3,1},{4,6},{5,7},{6,4},{7,5},{8,10},{9,11},{10,... | collective-permute-start | bytes 645128 | tf_op jit(solution)/shard_map/ppermute | solution.py:113
  96.4 9.4 %collective-permute-start.20 = (bf16[1,2,64,336]{3,2,1,0:T(8,128)(2,1)S(1)}, bf16[1,2,64,336]{3,2,1,0:T(8,128)(2,1)S(1)}, u32[]{:S(2)}, u32[]{:S(2)}) collective-permute-start(bf16[1,2,64,336]{3,2,1,0:T(8,128)(2,1)S(1)} %constant_dynamic-slice_fusion.2), channel_id=1, source_target_pairs={{0,2},{1,3},{2,0},{3,1},{4,6},{5,7},{6,4},{7,5},{8,10},{9,11},{10,... | collective-permute-start | bytes 258056 | tf_op jit(solution)/shard_map/ppermute | solution.py:113
  113.8 12.1 %collective-permute-start.25 = (bf16[64,2816]{1,0:T(8,128)(2,1)}, bf16[64,2816]{1,0:T(8,128)(2,1)S(1)}, u32[]{:S(2)}, u32[]{:S(2)}) collective-permute-start(bf16[64,2816]{1,0:T(8,128)(2,1)} %fusion.145), channel_id=1, source_target_pairs={{0,8},{1,9},{2,10},{3,11},{4,12},{5,13},{6,14},{7,15},{8,0},{9,1},... | collective-permute-start | bytes 1081352 | tf_op jit(solution)/shard_map/ppermute | solution.py:121
  115.9 7.4 %collective-permute-start.26 = (bf16[32,2688]{1,0:T(8,128)(2,1)S(1)}, bf16[32,2688]{1,0:T(8,128)(2,1)S(1)}, u32[]{:S(2)}, u32[]{:S(2)}) collective-permute-start(bf16[32,2688]{1,0:T(8,128)(2,1)S(1)} %convolution_convert_fusion.17), channel_id=1, source_target_pairs={{0,2},{1,3},{2,0},{3,1},{4,6},{5,7},{6,4},{7,5},{8,10},{9,11},{10,... | collective-permute-start | bytes 516104 | tf_op jit(solution)/shard_map/ppermute | solution.py:121
  117.2 6.2 %collective-permute-start.27 = (bf16[32,2688]{1,0:T(8,128)(2,1)S(1)}, bf16[32,2688]{1,0:T(8,128)(2,1)S(1)}, u32[]{:S(2)}, u32[]{:S(2)}) collective-permute-start(bf16[32,2688]{1,0:T(8,128)(2,1)S(1)} %convolution_convert_fusion.16), channel_id=1, source_target_pairs={{0,4},{1,5},{2,6},{3,7},{4,0},{5,1},{6,2},{7,3},{8,12},{9,13},{10,... | collective-permute-start | bytes 516104 | tf_op jit(solution)/shard_map/ppermute | solution.py:121
  118.7 7.3 %collective-permute-start.28 = (bf16[32,2688]{1,0:T(8,128)(2,1)S(1)}, bf16[32,2688]{1,0:T(8,128)(2,1)S(1)}, u32[]{:S(2)}, u32[]{:S(2)}) collective-permute-start(bf16[32,2688]{1,0:T(8,128)(2,1)S(1)} %convolution_convert_fusion.15), channel_id=1, source_target_pairs={{0,6},{1,7},{2,4},{3,5},{4,2},{5,3},{6,0},{7,1},{8,14},{9,15},{10,... | collective-permute-start | bytes 516104 | tf_op jit(solution)/shard_map/ppermute | solution.py:121
  118.9 26.7 %collective-permute-start.30 = (bf16[64,2816]{1,0:T(8,128)(2,1)}, bf16[64,2816]{1,0:T(8,128)(2,1)S(1)}, u32[]{:S(2)}, u32[]{:S(2)}) collective-permute-start(bf16[64,2816]{1,0:T(8,128)(2,1)} %fusion.145), channel_id=1, source_target_pairs={{0,16},{1,17},{2,18},{3,19},{4,20},{5,21},{6,22},{7,23},{8,24},{9,... | collective-permute-start | bytes 1081352 | tf_op jit(solution)/shard_map/ppermute | solution.py:121
  137.1 6.7 %collective-permute-start.35 = (bf16[128,2688]{1,0:T(8,128)(2,1)S(1)}, bf16[128,2688]{1,0:T(8,128)(2,1)S(1)}, u32[]{:S(2)}, u32[]{:S(2)}) collective-permute-start(bf16[128,2688]{1,0:T(8,128)(2,1)S(1)} %slice.481), channel_id=1, source_target_pairs={{0,1},{1,0},{2,3},{3,2},{4,5},{5,4},{6,7},{7,6},{8,9},{9,8},{10,11... | collective-permute-start | bytes 2064392 | tf_op jit(solution)/shard_map/ppermute | solution.py:121
  137.9 29.5 %collective-permute-start.29 = (bf16[64,2816]{1,0:T(8,128)(2,1)}, bf16[64,2816]{1,0:T(8,128)(2,1)S(1)}, u32[]{:S(2)}, u32[]{:S(2)}) collective-permute-start(bf16[64,2816]{1,0:T(8,128)(2,1)} %fusion.145), channel_id=1, source_target_pairs={{0,24},{1,25},{2,26},{3,27},{4,28},{5,29},{6,30},{7,31},{8,16},{9,... | collective-permute-start | bytes 1081352 | tf_op jit(solution)/shard_map/ppermute | solution.py:121
  143.8 7.6 %collective-permute-start.33 = (bf16[32,2688]{1,0:T(8,128)(2,1)S(1)}, bf16[32,2688]{1,0:T(8,128)(2,1)S(1)}, u32[]{:S(2)}, u32[]{:S(2)}) collective-permute-start(bf16[32,2688]{1,0:T(8,128)(2,1)S(1)} %convolution_convert_fusion.11), channel_id=1, source_target_pairs={{0,6},{1,7},{2,4},{3,5},{4,2},{5,3},{6,0},{7,1},{8,14},{9,15},{10,... | collective-permute-start | bytes 516104 | tf_op jit(solution)/shard_map/ppermute | solution.py:121
  163.0 7.7 %collective-permute-start.40 = (bf16[128,2688]{1,0:T(8,128)(2,1)S(1)}, bf16[128,2688]{1,0:T(8,128)(2,1)S(1)}, u32[]{:S(2)}, u32[]{:S(2)}) collective-permute-start(bf16[128,2688]{1,0:T(8,128)(2,1)S(1)} %slice.491), channel_id=1, source_target_pairs={{0,1},{1,0},{2,3},{3,2},{4,5},{5,4},{6,7},{7,6},{8,9},{9,8},{10,11... | collective-permute-start | bytes 2064392 | tf_op jit(solution)/shard_map/ppermute | solution.py:121
  164.1 5.9 %collective-permute-start.36 = (bf16[32,2688]{1,0:T(8,128)(2,1)S(1)}, bf16[32,2688]{1,0:T(8,128)(2,1)S(1)}, u32[]{:S(2)}, u32[]{:S(2)}) collective-permute-start(bf16[32,2688]{1,0:T(8,128)(2,1)S(1)} %convolution_convert_fusion.9), channel_id=1, source_target_pairs={{0,2},{1,3},{2,0},{3,1},{4,6},{5,7},{6,4},{7,5},{8,10},{9,11},{10,... | collective-permute-start | bytes 516104 | tf_op jit(solution)/shard_map/ppermute | solution.py:121
  165.5 6.9 %collective-permute-start.37 = (bf16[32,2688]{1,0:T(8,128)(2,1)S(1)}, bf16[32,2688]{1,0:T(8,128)(2,1)S(1)}, u32[]{:S(2)}, u32[]{:S(2)}) collective-permute-start(bf16[32,2688]{1,0:T(8,128)(2,1)S(1)} %convolution_convert_fusion.8), channel_id=1, source_target_pairs={{0,4},{1,5},{2,6},{3,7},{4,0},{5,1},{6,2},{7,3},{8,12},{9,13},{10,... | collective-permute-start | bytes 516104 | tf_op jit(solution)/shard_map/ppermute | solution.py:121
  166.2 8.0 %collective-permute-start.38 = (bf16[32,2688]{1,0:T(8,128)(2,1)S(1)}, bf16[32,2688]{1,0:T(8,128)(2,1)S(1)}, u32[]{:S(2)}, u32[]{:S(2)}) collective-permute-start(bf16[32,2688]{1,0:T(8,128)(2,1)S(1)} %convolution_convert_fusion.7), channel_id=1, source_target_pairs={{0,6},{1,7},{2,4},{3,5},{4,2},{5,3},{6,0},{7,1},{8,14},{9,15},{10,... | collective-permute-start | bytes 516104 | tf_op jit(solution)/shard_map/ppermute | solution.py:121
  167.4 10.0 %collective-permute-start.41 = (bf16[32,2688]{1,0:T(8,128)(2,1)S(1)}, bf16[32,2688]{1,0:T(8,128)(2,1)S(1)}, u32[]{:S(2)}, u32[]{:S(2)}) collective-permute-start(bf16[32,2688]{1,0:T(8,128)(2,1)S(1)} %get-tuple-element.223), channel_id=1, source_target_pairs={{0,2},{1,3},{2,0},{3,1},{4,6},{5,7},{6,4},{7,5},{8,10},{9,11},{10,... | collective-permute-start | bytes 516104 | tf_op jit(solution)/shard_map/ppermute | solution.py:121
  170.0 9.2 %collective-permute-start.42 = (bf16[32,2688]{1,0:T(8,128)(2,1)S(1)}, bf16[32,2688]{1,0:T(8,128)(2,1)S(1)}, u32[]{:S(2)}, u32[]{:S(2)}) collective-permute-start(bf16[32,2688]{1,0:T(8,128)(2,1)S(1)} %get-tuple-element.222), channel_id=1, source_target_pairs={{0,4},{1,5},{2,6},{3,7},{4,0},{5,1},{6,2},{7,3},{8,12},{9,13},{10,... | collective-permute-start | bytes 516104 | tf_op jit(solution)/shard_map/ppermute | solution.py:121
  170.7 10.9 %collective-permute-start.43 = (bf16[32,2688]{1,0:T(8,128)(2,1)S(1)}, bf16[32,2688]{1,0:T(8,128)(2,1)S(1)}, u32[]{:S(2)}, u32[]{:S(2)}) collective-permute-start(bf16[32,2688]{1,0:T(8,128)(2,1)S(1)} %get-tuple-element.221), channel_id=1, source_target_pairs={{0,6},{1,7},{2,4},{3,5},{4,2},{5,3},{6,0},{7,1},{8,14},{9,15},{10,... | collective-permute-start | bytes 516104 | tf_op jit(solution)/shard_map/ppermute | solution.py:121
  184.3 16.1 %collective-permute-start.44 = (bf16[32,2688]{1,0:T(8,128)(2,1)S(1)}, bf16[32,2688]{1,0:T(8,128)(2,1)S(1)}, u32[]{:S(2)}, u32[]{:S(2)}) collective-permute-start(bf16[32,2688]{1,0:T(8,128)(2,1)S(1)} %convolution_convert_fusion.5), channel_id=1, source_target_pairs={{0,2},{1,3},{2,0},{3,1},{4,6},{5,7},{6,4},{7,5},{8,10},{9,11},{10,... | collective-permute-start | bytes 516104 | tf_op jit(solution)/shard_map/ppermute | solution.py:121
  185.2 17.6 %collective-permute-start.45 = (bf16[32,2688]{1,0:T(8,128)(2,1)S(1)}, bf16[32,2688]{1,0:T(8,128)(2,1)S(1)}, u32[]{:S(2)}, u32[]{:S(2)}) collective-permute-start(bf16[32,2688]{1,0:T(8,128)(2,1)S(1)} %convolution_convert_fusion.4), channel_id=1, source_target_pairs={{0,4},{1,5},{2,6},{3,7},{4,0},{5,1},{6,2},{7,3},{8,12},{9,13},{10,... | collective-permute-start | bytes 516104 | tf_op jit(solution)/shard_map/ppermute | solution.py:121
  186.1 16.8 %collective-permute-start.46 = (bf16[32,2688]{1,0:T(8,128)(2,1)S(1)}, bf16[32,2688]{1,0:T(8,128)(2,1)S(1)}, u32[]{:S(2)}, u32[]{:S(2)}) collective-permute-start(bf16[32,2688]{1,0:T(8,128)(2,1)S(1)} %convolution_convert_fusion.3), channel_id=1, source_target_pairs={{0,6},{1,7},{2,4},{3,5},{4,2},{5,3},{6,0},{7,1},{8,14},{9,15},{10,... | collective-permute-start | bytes 516104 | tf_op jit(solution)/shard_map/ppermute | solution.py:121
  201.5 8.2 %collective-permute-start.51 = (bf16[32,2688]{1,0:T(8,128)(2,1)S(1)}, bf16[32,2688]{1,0:T(8,128)(2,1)S(1)}, u32[]{:S(2)}, u32[]{:S(2)}) collective-permute-start(bf16[32,2688]{1,0:T(8,128)(2,1)S(1)} %get-tuple-element.217), channel_id=1, source_target_pairs={{0,6},{1,7},{2,4},{3,5},{4,2},{5,3},{6,0},{7,1},{8,14},{9,15},{10,... | collective-permute-start | bytes 516104 | tf_op jit(solution)/shard_map/ppermute | solution.py:121
  216.8 6.8 %collective-permute-start.55 = (bf16[32,2688]{1,0:T(8,128)(2,1)S(1)}, bf16[32,2688]{1,0:T(8,128)(2,1)S(1)}, u32[]{:S(2)}, u32[]{:S(2)}) collective-permute-start(bf16[32,2688]{1,0:T(8,128)(2,1)S(1)} %get-tuple-element.210), channel_id=1, source_target_pairs={{0,6},{1,7},{2,4},{3,5},{4,2},{5,3},{6,0},{7,1},{8,14},{9,15},{10,... | collective-permute-start | bytes 516104 | tf_op jit(solution)/shard_map/ppermute | solution.py:121
  218.2 10.0 %collective-permute-start.54 = (bf16[32,2688]{1,0:T(8,128)(2,1)S(1)}, bf16[32,2688]{1,0:T(8,128)(2,1)S(1)}, u32[]{:S(2)}, u32[]{:S(2)}) collective-permute-start(bf16[32,2688]{1,0:T(8,128)(2,1)S(1)} %get-tuple-element.211), channel_id=1, source_target_pairs={{0,4},{1,5},{2,6},{3,7},{4,0},{5,1},{6,2},{7,3},{8,12},{9,13},{10,... | collective-permute-start | bytes 516104 | tf_op jit(solution)/shard_map/ppermute | solution.py:121
  219.1 10.2 %collective-permute-start.53 = (bf16[32,2688]{1,0:T(8,128)(2,1)S(1)}, bf16[32,2688]{1,0:T(8,128)(2,1)S(1)}, u32[]{:S(2)}, u32[]{:S(2)}) collective-permute-start(bf16[32,2688]{1,0:T(8,128)(2,1)S(1)} %get-tuple-element.212), channel_id=1, source_target_pairs={{0,2},{1,3},{2,0},{3,1},{4,6},{5,7},{6,4},{7,5},{8,10},{9,11},{10,... | collective-permute-start | bytes 516104 | tf_op jit(solution)/shard_map/ppermute | solution.py:121
  219.7 15.8 %collective-permute-start.52 = (bf16[64,2688]{1,0:T(8,128)(2,1)S(1)}, bf16[64,2688]{1,0:T(8,128)(2,1)S(1)}, u32[]{:S(2)}, u32[]{:S(2)}) collective-permute-start(bf16[64,2688]{1,0:T(8,128)(2,1)S(1)} %convolution_convert_fusion.2), channel_id=1, source_target_pairs={{0,8},{1,9},{2,10},{3,11},{4,12},{5,13},{6,14},{7,15},{8,0},{9,1},... | collective-permute-start | bytes 1032200 | tf_op jit(solution)/shard_map/ppermute | solution.py:121
  221.9 9.1 %collective-permute-start.61 = (bf16[32,2688]{1,0:T(8,128)(2,1)S(1)}, bf16[32,2688]{1,0:T(8,128)(2,1)S(1)}, u32[]{:S(2)}, u32[]{:S(2)}) collective-permute-start(bf16[32,2688]{1,0:T(8,128)(2,1)S(1)} %get-tuple-element.214), channel_id=1, source_target_pairs={{0,6},{1,7},{2,4},{3,5},{4,2},{5,3},{6,0},{7,1},{8,14},{9,15},{10,... | collective-permute-start | bytes 516104 | tf_op jit(solution)/shard_map/ppermute | solution.py:121
  223.6 11.5 %collective-permute-start.60 = (bf16[32,2688]{1,0:T(8,128)(2,1)S(1)}, bf16[32,2688]{1,0:T(8,128)(2,1)S(1)}, u32[]{:S(2)}, u32[]{:S(2)}) collective-permute-start(bf16[32,2688]{1,0:T(8,128)(2,1)S(1)} %get-tuple-element.215), channel_id=1, source_target_pairs={{0,4},{1,5},{2,6},{3,7},{4,0},{5,1},{6,2},{7,3},{8,12},{9,13},{10,... | collective-permute-start | bytes 516104 | tf_op jit(solution)/shard_map/ppermute | solution.py:121
  228.2 6.9 %collective-permute-start.59 = (bf16[32,2688]{1,0:T(8,128)(2,1)S(1)}, bf16[32,2688]{1,0:T(8,128)(2,1)S(1)}, u32[]{:S(2)}, u32[]{:S(2)}) collective-permute-start(bf16[32,2688]{1,0:T(8,128)(2,1)S(1)} %get-tuple-element.216), channel_id=1, source_target_pairs={{0,2},{1,3},{2,0},{3,1},{4,6},{5,7},{6,4},{7,5},{8,10},{9,11},{10,... | collective-permute-start | bytes 516104 | tf_op jit(solution)/shard_map/ppermute | solution.py:121
  229.5 23.5 %collective-permute-start.56 = (bf16[64,2688]{1,0:T(8,128)(2,1)S(1)}, bf16[64,2688]{1,0:T(8,128)(2,1)S(1)}, u32[]{:S(2)}, u32[]{:S(2)}) collective-permute-start(bf16[64,2688]{1,0:T(8,128)(2,1)S(1)} %convolution_convert_fusion.1), channel_id=1, source_target_pairs={{0,16},{1,17},{2,18},{3,19},{4,20},{5,21},{6,22},{7,23},{8,24},{9,... | collective-permute-start | bytes 1032200 | tf_op jit(solution)/shard_map/ppermute | solution.py:121
  235.4 27.0 %collective-permute-start.62 = (bf16[64,2688]{1,0:T(8,128)(2,1)S(1)}, bf16[64,2688]{1,0:T(8,128)(2,1)S(1)}, u32[]{:S(2)}, u32[]{:S(2)}) collective-permute-start(bf16[64,2688]{1,0:T(8,128)(2,1)S(1)} %convolution_convert_fusion), channel_id=1, source_target_pairs={{0,24},{1,25},{2,26},{3,27},{4,28},{5,29},{6,30},{7,31},{8,16},{9,... | collective-permute-start | bytes 1032200 | tf_op jit(solution)/shard_map/ppermute | solution.py:121
  (56 other events, 301.9 us)

commit v2 on v0

--- a/solution.py
+++ b/solution.py
@@ -26,7 +26,9 @@
 
 
 def pick(parts, index):
-    return lax.dynamic_index_in_dim(parts, index, 0, keepdims=False)
+    return lax.dynamic_index_in_dim(
+        parts, index, 0, keepdims=False, allow_negative_indices=False
+    )
 
 
 def packed(state, decay):
@@ -45,7 +47,7 @@
 
 
 def swapped(decay, state, axis):
-    size, side = lax.axis_size(axis), lax.axis_index(axis) % 2
+    size, side = lax.axis_size(axis), lax.axis_index(axis) & 1
     half = decay.shape[0] // 2
     states = state.reshape(2, half, HEAD_DIM, STATE)
     decays = decay.reshape(2, half)
@@ -57,27 +59,35 @@
 
 
 def entering(got, decay, state, axis):
-    size, side = lax.axis_size(axis), lax.axis_index(axis) % 2
+    size, side = lax.axis_size(axis), lax.axis_index(axis) & 1
     odd = side == 1
     half = decay.shape[0] // 2
     other_state, other_decay = unpacked(got, half)
     own_state = pick(state.reshape(2, half, HEAD_DIM, STATE), side)
     own_decay = pick(decay.reshape(2, half), side)
     first_state = jnp.where(odd, other_state, own_state)
-    second_state = jnp.where(odd, own_state, other_state)
     first_decay = jnp.where(odd, other_decay, own_decay)
     second_decay = jnp.where(odd, own_decay, other_decay)
-    pair = packed(
-        second_decay[:, None, None] * first_state + second_state, first_decay * second_decay
-    )
-    before = jnp.zeros_like(first_state)
-    received = [
-        lax.ppermute(pair, axis, [(i, i + 2 * d) for i in range(size - 2 * d)])
-        for d in range(1, size // 2)
-    ]
-    for block in received[::-1]:
-        block_state, block_decay = unpacked(block, half)
-        before = block_decay[:, None, None] * before + block_state
+    total_state = second_decay[:, None, None] * first_state + jnp.where(
+        odd, own_state, other_state
+    )
+    total_decay = first_decay * second_decay
+    before, before_decay = jnp.zeros_like(first_state), jnp.ones_like(first_decay)
+    stride = 2
+    while stride < size:
+        later = (lax.axis_index(axis) & stride) != 0
+        came = lax.ppermute(
+            packed(total_state, total_decay), axis, [(i, i ^ stride) for i in range(size)]
+        )
+        came_state, came_decay = unpacked(came, half)
+        before = jnp.where(later, before_decay[:, None, None] * came_state + before, before)
+        before_decay = jnp.where(later, before_decay * came_decay, before_decay)
+        early_state = jnp.where(later, came_state, total_state)
+        late_state = jnp.where(later, total_state, came_state)
+        late_decay = jnp.where(later, total_decay, came_decay)
+        total_state = late_decay[:, None, None] * early_state + late_state
+        total_decay = total_decay * came_decay
+        stride *= 2
     inner = first_decay[:, None, None] * before + first_state
     mine_half = jnp.where(odd, inner, before)
     send_half = jnp.where(odd, before, inner).astype(jnp.bfloat16)
@@ -94,22 +104,28 @@
     size = lax.axis_size(axis)
     order = seq_ring(size)
     ahead, behind = parts
-    if 2 * step < size:
-        ahead = tuple(shift(part, axis, order, 1) for part in ahead)
-        behind = tuple(shift(part, axis, order, -1) for part in behind)
-        return ahead, behind
-    return (shift(ahead[0], axis, order, 1),), (shift(behind[1], axis, order, -1),)
+    last = 2 * step >= size
+    first = [shift(ahead[0], axis, order, 1)] + ([] if last else [shift(behind[0], axis, order, -1)])
+    second = [shift(behind[1], axis, order, -1)] + ([] if last else [shift(ahead[1], axis, order, 1)])
+    if last:
+        return (first[0],), (second[0],)
+    return (first[0], second[1]), (first[1], second[0])
 
 
 def head_scatter(pieces, axis):
     size, mine = lax.axis_size(axis), lax.axis_index(axis)
     stride = 1
     while stride < size:
-        bit = (mine // stride) % 2
+        bit = (mine & stride) != 0
+        bit = bit.astype(jnp.int32)
         left = pieces.shape[0] // 2
         view = pieces.reshape(left, 2, *pieces.shape[1:])
-        send = lax.dynamic_index_in_dim(view, 1 - bit, 1, keepdims=False)
-        keep = lax.dynamic_index_in_dim(view, bit, 1, keepdims=False)
+        send = lax.dynamic_index_in_dim(
+            view, 1 - bit, 1, keepdims=False, allow_negative_indices=False
+        )
+        keep = lax.dynamic_index_in_dim(
+            view, bit, 1, keepdims=False, allow_negative_indices=False
+        )
         came = lax.ppermute(send, axis, [(i, i ^ stride) for i in range(size)])
         pieces = (keep.astype(jnp.float32) + came.astype(jnp.float32)).astype(jnp.bfloat16)
         stride *= 2
@@ -172,7 +188,9 @@
         values_in, steps_in, write_in, read_in = pieces
         log_decay = -steps_in * decay_rates[None, :]
         cumulative = jnp.cumsum(log_decay, axis=0)
-        scores = jnp.einsum("tgn,sgn->gts", read_in, write_in, preferred_element_type=jnp.float32)
+        scores = jnp.einsum(
+            "tgn,sgn->gts", read_in, write_in, preferred_element_type=jnp.float32
+        )
         scores = jnp.repeat(scores, per_group, axis=0)
         decays = jnp.exp(cumulative.T[:, :, None] - cumulative.T[:, None, :])
         mixing = jnp.where(causal[None], scores * decays * steps_in.T[:, None, :], 0.0).astype(
@@ -208,7 +226,6 @@
     )
 
     got = swapped(device_decay, device_state, "seq")
-    ring[0], got = lax.optimization_barrier((ring[0], got))
     for step in range(2, seq_size // 2 + 1):
         ring.append(ring_step(ring[-1], "seq", step))
     incoming = entering(got, device_decay, device_state, "seq")
@@ -225,7 +242,9 @@
         carried = carried * jnp.exp(cumulative)[:, :, None]
         return (jnp.exp(block_total)[:, None, None] * carry_state + fresh_state, carried)
 
-    _, carried_all = lax.scan(emit_rows, incoming, (reads, cumul_all, totals_blk, fresh_all))
+    _, carried_all = lax.scan(
+        emit_rows, incoming, (reads, cumul_all, totals_blk, fresh_all)
+    )
     values_flat = ssm_values.reshape(tokens_dev, heads_dev, HEAD_DIM).astype(jnp.float32)
     ssm_out = (inner_all + carried_all).reshape(tokens_dev, heads_dev, HEAD_DIM) + skip_gain[
         None, :, None
@@ -255,19 +274,21 @@
         ahead, behind = ring[step - 1]
         offsets += [-step, step] if 2 * step < seq_size else [-step]
         products += product([*ahead, *behind])
-        if step in (seq_size // 4, seq_size // 2):
+        if step in (seq_size // 4, seq_size // 2 - 1, seq_size // 2):
             batches.append(head_scatter(jnp.concatenate(products, axis=1), "head"))
             products = []
-    scattered = jnp.concatenate(batches, axis=0).astype(jnp.float32)
+    scattered = jnp.concatenate(batches, axis=0)
+    came = {step % seq_size: at for at, step in enumerate(offsets)}
+    in_order = jnp.concatenate([scattered[came[step] : came[step] + 1] for step in range(seq_size)] * 2, axis=0)
+    index = lax.axis_index("seq")
+    ring_place = jnp.where((index & 1) == 0, index >> 1, seq_size - 1 - (index >> 1))
+    on_ring = lax.dynamic_slice_in_dim(
+        in_order, seq_size - ring_place, seq_size, allow_negative_indices=False
+    )
     order = seq_ring(seq_size)
-    table = [[0] * seq_size for _ in range(seq_size)]
-    for place, index in enumerate(order):
-        for at, step in enumerate(offsets):
-            table[index][order[(place + step) % seq_size]] = at
-    places = jnp.asarray(table, jnp.int32)[lax.axis_index("seq")]
     mixed_out = jnp.concatenate(
-        [pick(scattered, places[b]) for b in range(seq_size)], axis=1
-    )
+        [on_ring[order.index(b)] for b in range(seq_size)], axis=1
+    ).astype(jnp.float32)
     hidden = residual.astype(jnp.float32) + mixed_out
     inputs = (
         hidden
@@ -277,7 +298,9 @@
     logits = jnp.dot(inputs, router_weight, preferred_element_type=jnp.float32)
     experts = router_weight.shape[1]
     model_width = inputs.shape[1]
-    expert_hits = expert_index[:, :, None] == jnp.arange(experts, dtype=jnp.int32)[None, None, :]
+    expert_hits = (
+        expert_index[:, :, None] == jnp.arange(experts, dtype=jnp.int32)[None, None, :]
+    )
     picked = jnp.sum(jnp.where(expert_hits, logits[:, None, :], 0.0), axis=-1)
     probability = jax.nn.sigmoid(picked)
     shares = ROUTE_SCALE * probability / jnp.sum(probability, axis=1, keepdims=True)
@@ -300,10 +323,12 @@
     inner = experts // 4
     stride = 2 * inner
     place = lax.axis_index("seq") * lax.axis_size("head") + lax.axis_index("head")
-    mine_outer, mine_inner = place // stride, place // 2 % inner
+    mine_inner = (place >> 1) & (inner - 1)
     turned = mine_inner ^ jnp.arange(inner, dtype=jnp.int32)
-    wanted = (mine_outer * inner + turned)[:, None] * capacity + jnp.arange(capacity, dtype=jnp.int32)
+    wanted = ((place >> 1) - mine_inner + turned)[:, None] * capacity + jnp.arange(capacity, dtype=jnp.int32)
     wanted = wanted.reshape(-1).astype(jnp.float32)
+
+    turns = (0, 2, 3, 1)
 
     def placed(rows):
         notes = rows[:, width : width + 3 * TOP].astype(jnp.float32)
@@ -313,19 +338,26 @@
         weights = jnp.sum(jnp.where(match, notes[:, 2 * TOP :, None], 0.0), axis=1)
         return placing, weights.astype(jnp.bfloat16)
 
-    def spread(rows):
+    def spread(rows, summed=None):
         placing, weights = placed(rows)
         inputs = rows[:, :width]
-        parts = []
+        parts, results = [], []
         for m in range(inner):
+            here = slice(m * capacity, (m + 1) * capacity)
             part = lax.dot_general(
-                placing[:, m * capacity : (m + 1) * capacity],
+                placing[:, here],
                 inputs,
                 (((0,), (0,)), ((), ())),
                 preferred_element_type=jnp.float32,
             ).astype(jnp.bfloat16)
-            parts.append(across(part, 2 * m) if m else part)
-        return parts, weights
+            result = None if summed is None else summed[here]
+            if m:
+                both = part if summed is None else jnp.concatenate([part, result], axis=0)
+                both = across(both, 2 * m)
+                part, result = both[:capacity], both[capacity:]
+            parts.append(part)
+            results.append(result)
+        return parts, weights, results
 
     def expert(parts):
         own_rows = jnp.concatenate(parts, axis=0)
@@ -347,35 +379,33 @@
         partial = jnp.dot(
             weights, jnp.concatenate(results, axis=0), preferred_element_type=jnp.float32
         )
-        return across(partial.astype(jnp.bfloat16), k * stride) if k else partial
+        return across(partial.astype(jnp.bfloat16), turns[k] * stride) if k else partial
 
     def line(k):
-        return across(block, k * stride)
+        return across(block, turns[k] * stride)
 
     rows1 = line(1)
     sent0 = spread(block)
-    rows1, sent0, block = lax.optimization_barrier((rows1, sent0, block))
+    rows1, sent0, block = lax.optimization_barrier((rows1, sent0[:2], block))
 
     rows2 = line(2)
     sent1 = spread(rows1)
     done0 = expert(sent0[0])
-    rows2, sent1, done0, block = lax.optimization_barrier((rows2, sent1, done0, block))
+    rows2, sent1, done0, block = lax.optimization_barrier((rows2, sent1[:2], done0, block))
 
     rows3 = line(3)
-    sent2 = spread(rows2)
+    sent2 = spread(rows2, done0)
     done1 = expert(sent1[0])
-    back0 = brought(done0)
-    rows3, sent2, done1, back0 = lax.optimization_barrier((rows3, sent2, done1, back0))
-
-    sent3 = spread(rows3)
+    rows3, sent2, done1 = lax.optimization_barrier((rows3, sent2, done1))
+
+    sent3 = spread(rows3, done1)
     done2 = expert(sent2[0])
-    back1 = brought(done1)
-    sum0 = home(back0, sent0[1], 0)
-    sent3, done2, back1, sum0 = lax.optimization_barrier((sent3, done2, back1, sum0))
+    sum0 = home(sent2[2], sent0[1], 0)
+    sent3, done2, sum0 = lax.optimization_barrier((sent3, done2, sum0))
 
     done3 = expert(sent3[0])
     back2 = brought(done2)
-    sum1 = home(back1, sent1[1], 1)
+    sum1 = home(sent3[2], sent1[1], 1)
     back3 = brought(done3)
     sum2 = home(back2, sent2[1], 2)
     sum3 = home(back3, sent3[1], 3)

time: 265 us -> 234 us (0.88)
  the two profiles are of different devices: /device:TPU:9 before, /device:TPU:0 now
where the time goes in v2:
time: 234 us
  waiting for transfers between devices  108 us (46%)
  starting transfers between devices  53.5 us (23%)
  matrix products  37.7 us (16%)
  local copies, waits for them, and re-layouts  20.7 us (9%)
  other arithmetic  12.2 us (5%)
    ppermute x32, waiting for transfers between devices, across(): lax.ppermute(x, axes, [(i, i ^ mask) for i in range(lax.axis_size(axes))])  62 us
    ppermute x32, starting transfers between devices, across(): lax.ppermute(x, axes, [(i, i ^ mask) for i in range(lax.axis_size(axes))])  32.1 us
    dot_general x4, matrix products, expert_half(): jnp.dot(flat_rows, up_weight[0], preferred_element_type=jnp.float32)  13.9 us
    ppermute x14, starting transfers between devices, shift(): lax.ppermute(x, axis, [(order[i], order[(i + step) % size]) for i in rang...  13.9 us
    ppermute x6, waiting for transfers between devices, head_scatter(): came = lax.ppermute(send, axis, [(i, i ^ stride) for i in range(size)])  12.8 us
    ppermute x14, waiting for transfers between devices, shift(): lax.ppermute(x, axis, [(order[i], order[(i + step) % size]) for i in rang...  10.9 us
    ppermute x1, waiting for transfers between devices, entering(): lax.ppermute(send_half.reshape(-1, STATE), axis, [(i, i ^ 1) for i in ran...  10.9 us
    ppermute x2, waiting for transfers between devices, entering(): lax.ppermute(packed(total_state, total_decay), axis, [(i, i ^ stride) for...  8.37 us
  transfers between devices with their start and end apart: 56, of which 28 were waited for; matrix products, arithmetic and copies ran while one was open for 21% of the time, Pallas kernels for 0%

profile of v2, /device:TPU:0, one launch (start us, length us, event | category | flops | bytes accessed | tf_op | source)
XLA Modules:
  0.0 233.5 jit_solution(4703336651448885301)
XLA Ops:
  0.0 1.8 slice.561
  1.8 3.0 %collective-permute-start.7 = (bf16[160,1024]{1,0:T(8,128)(2,1)}, bf16[160,1024]{1,0:T(8,128)(2,1)}, u32[]{:S(2)}, u32[]{:S(2)}) collective-permute-start(bf16[160,1024]{1,0:T(8,128)(2,1)} %slice.561), channel_id=1, source_target_pairs={{0,4},{8,0},{16,8},{24,16},{28,24},{20,28},{12,20},{4,12},{1,5},{9... | collective-permute-start | bytes 983048 | tf_op jit(solution)/shard_map/ppermute | solution.py:25
  4.9 1.7 slice.560
  6.6 2.0 collective-permute-start.6
  11.7 2.0 collective-permute-start
  15.6 1.8 convolution_bitcast_fusion
  22.2 2.6 %collective-permute-done = bf16[528,128]{1,0:T(8,128)(2,1)S(1)} collective-permute-done((bf16[528,128]{1,0:T(8,128)(2,1)S(1)}, bf16[528,128]{1,0:T(8,128)(2,1)S(1)}, u32[]{:S(2)}, u32[]{:S(2)}) %collective-permute-start) | collective-permute-done | bytes 135200 | tf_op jit(solution)/shard_map/ppermute | solution.py:54
  25.5 4.8 %collective-permute-done.1 = bf16[528,128]{1,0:T(8,128)(2,1)S(1)} collective-permute-done((bf16[528,128]{1,0:T(8,128)(2,1)S(1)}, bf16[528,128]{1,0:T(8,128)(2,1)S(1)}, u32[]{:S(2)}, u32[]{:S(2)}) %collective-permute-start.1) | collective-permute-done | bytes 135200 | tf_op jit(solution)/shard_map/ppermute | solution.py:79
  32.7 1.7 collective-permute-start.11
  34.7 1.7 collective-permute-start.10
  36.8 3.5 %collective-permute-done.2 = bf16[528,128]{1,0:T(8,128)(2,1)S(1)} collective-permute-done((bf16[528,128]{1,0:T(8,128)(2,1)}, bf16[528,128]{1,0:T(8,128)(2,1)S(1)}, u32[]{:S(2)}, u32[]{:S(2)}) %collective-permute-start.2) | collective-permute-done | bytes 135200 | tf_op jit(solution)/shard_map/ppermute | solution.py:79
  41.2 10.9 %collective-permute-done.3 = bf16[512,128]{1,0:T(8,128)(2,1)S(1)} collective-permute-done((bf16[512,128]{1,0:T(8,128)(2,1)S(1)}, bf16[512,128]{1,0:T(8,128)(2,1)S(1)}, u32[]{:S(2)}, u32[]{:S(2)}) %collective-permute-start.3) | collective-permute-done | bytes 131104 | tf_op jit(solution)/shard_map/ppermute | solution.py:94
  53.6 1.7 fusion.106
  59.2 1.9 fusion.99
  62.1 1.8 collective-permute-start.15
  63.8 1.9 fusion.96
  66.4 1.8 collective-permute-start.14
  68.5 4.2 %collective-permute-done.17 = bf16[160,1024]{1,0:T(8,128)(2,1)} collective-permute-done((bf16[160,1024]{1,0:T(8,128)(2,1)}, bf16[160,1024]{1,0:T(8,128)(2,1)}, u32[]{:S(2)}, u32[]{:S(2)}) %collective-permute-start.17) | collective-permute-done | bytes 327712 | tf_op jit(solution)/shard_map/ppermute | solution.py:25
  73.0 6.7 %collective-permute-done.16 = bf16[176,1024]{1,0:T(8,128)(2,1)S(1)} collective-permute-done((bf16[176,1024]{1,0:T(8,128)(2,1)}, bf16[176,1024]{1,0:T(8,128)(2,1)S(1)}, u32[]{:S(2)}, u32[]{:S(2)}) %collective-permute-start.16) | collective-permute-done | bytes 360480 | tf_op jit(solution)/shard_map/ppermute | solution.py:25
  79.7 1.6 fusion.93
  85.6 3.5 %collective-permute-done.19 = bf16[1,2,64,336]{3,2,1,0:T(8,128)(2,1)S(1)} collective-permute-done((bf16[1,2,64,336]{3,2,1,0:T(8,128)(2,1)S(1)}, bf16[1,2,64,336]{3,2,1,0:T(8,128)(2,1)S(1)}, u32[]{:S(2)}, u32[]{:S(2)}) %collective-permute-start.19) | collective-permute-done | bytes 86048 | tf_op jit(solution)/shard_map/ppermute | solution.py:129
  89.1 4.4 %collective-permute-done.13 = bf16[1,5,64,336]{3,2,1,0:T(8,128)(2,1)S(1)} collective-permute-done((bf16[1,5,64,336]{3,2,1,0:T(8,128)(2,1)S(1)}, bf16[1,5,64,336]{3,2,1,0:T(8,128)(2,1)S(1)}, u32[]{:S(2)}, u32[]{:S(2)}) %collective-permute-start.13) | collective-permute-done | bytes 215072 | tf_op jit(solution)/shard_map/ppermute | solution.py:129
  98.2 2.6 %collective-permute-done.23 = bf16[1,1,64,336]{3,2,1,0:T(8,128)(2,1)S(1)} collective-permute-done((bf16[1,1,64,336]{3,2,1,0:T(8,128)(2,1)S(1)}, bf16[1,1,64,336]{3,2,1,0:T(8,128)(2,1)S(1)}, u32[]{:S(2)}, u32[]{:S(2)}) %collective-permute-start.23) | collective-permute-done | bytes 43040 | tf_op jit(solution)/shard_map/ppermute | solution.py:129
  108.3 2.4 %collective-permute-done.25 = bf16[32,2688]{1,0:T(8,128)(2,1)S(1)} collective-permute-done((bf16[32,2688]{1,0:T(8,128)(2,1)S(1)}, bf16[32,2688]{1,0:T(8,128)(2,1)S(1)}, u32[]{:S(2)}, u32[]{:S(2)}) %collective-permute-start.25) | collective-permute-done | bytes 172064 | tf_op jit(solution)/shard_map/ppermute | solution.py:137
  110.8 3.2 %collective-permute-done.26 = bf16[32,2688]{1,0:T(8,128)(2,1)S(1)} collective-permute-done((bf16[32,2688]{1,0:T(8,128)(2,1)S(1)}, bf16[32,2688]{1,0:T(8,128)(2,1)S(1)}, u32[]{:S(2)}, u32[]{:S(2)}) %collective-permute-start.26) | collective-permute-done | bytes 172064 | tf_op jit(solution)/shard_map/ppermute | solution.py:137
  114.0 6.4 %collective-permute-done.24 = bf16[64,2816]{1,0:T(8,128)(2,1)S(1)} collective-permute-done((bf16[64,2816]{1,0:T(8,128)(2,1)S(1)}, bf16[64,2816]{1,0:T(8,128)(2,1)S(1)}, u32[]{:S(2)}, u32[]{:S(2)}) %collective-permute-start.24) | collective-permute-done | bytes 360480 | tf_op jit(solution)/shard_map/ppermute | solution.py:137
  121.5 1.8 collective-permute-done.32
  123.3 4.1 %fusion.90 = bf16[256,928]{0,1:T(8,128)(2,1)S(1)} fusion(bf16[256,2688]{1,0:T(8,128)(2,1)S(1)} %constant_dynamic-update-slice_fusion.21, bf16[1,2688,928]{1,2,0:T(8,128)(2,1)} %param.40), kind=kOutput, calls=%fused_computation.88 | convolution fusion | flops 1277878272 | bytes 6840320 | tf_op jit(solution)/shard_map/dot_general | solution.py:143
  127.5 1.7 fusion.19
  129.8 2.0 collective-permute-start.28
  136.2 2.8 %collective-permute-done.29 = bf16[32,2688]{1,0:T(8,128)(2,1)S(1)} collective-permute-done((bf16[32,2688]{1,0:T(8,128)(2,1)S(1)}, bf16[32,2688]{1,0:T(8,128)(2,1)S(1)}, u32[]{:S(2)}, u32[]{:S(2)}) %collective-permute-start.29) | collective-permute-done | bytes 172064 | tf_op jit(solution)/shard_map/ppermute | solution.py:137
  139.0 4.0 %collective-permute-done.30 = bf16[32,2688]{1,0:T(8,128)(2,1)S(1)} collective-permute-done((bf16[32,2688]{1,0:T(8,128)(2,1)S(1)}, bf16[32,2688]{1,0:T(8,128)(2,1)S(1)}, u32[]{:S(2)}, u32[]{:S(2)}) %collective-permute-start.30) | collective-permute-done | bytes 172064 | tf_op jit(solution)/shard_map/ppermute | solution.py:137
  145.8 3.0 %collective-permute-start.34 = (bf16[64,2816]{1,0:T(8,128)(2,1)}, bf16[64,2816]{1,0:T(8,128)(2,1)S(1)}, u32[]{:S(2)}, u32[]{:S(2)}) collective-permute-start(bf16[64,2816]{1,0:T(8,128)(2,1)} %copy-done.15), channel_id=1, source_target_pairs={{0,8},{1,9},{2,10},{3,11},{4,12},{5,13},{6,14},{7,15},{8,0},{9,1},... | collective-permute-start | bytes 1081352 | tf_op jit(solution)/shard_map/ppermute | solution.py:137
  154.1 6.6 %collective-permute-done.35 = bf16[64,2688]{1,0:T(8,128)(2,1)S(1)} collective-permute-done((bf16[64,2688]{1,0:T(8,128)(2,1)S(1)}, bf16[64,2688]{1,0:T(8,128)(2,1)S(1)}, u32[]{:S(2)}, u32[]{:S(2)}) %collective-permute-start.35) | collective-permute-done | bytes 344096 | tf_op jit(solution)/shard_map/ppermute | solution.py:137
  160.8 4.1 %fusion.87 = bf16[256,928]{0,1:T(8,128)(2,1)S(1)} fusion(bf16[256,2688]{1,0:T(8,128)(2,1)S(1)} %constant_dynamic-update-slice_fusion.26, bf16[1,2688,928]{1,2,0:T(8,128)(2,1)} %param.40), kind=kOutput, calls=%fused_computation.87 | convolution fusion | flops 1277878272 | bytes 6840320 | tf_op jit(solution)/shard_map/dot_general | solution.py:143
  164.9 1.7 fusion.22
  175.7 6.3 %collective-permute-done.40 = bf16[64,2688]{1,0:T(8,128)(2,1)S(1)} collective-permute-done((bf16[64,2688]{1,0:T(8,128)(2,1)S(1)}, bf16[64,2688]{1,0:T(8,128)(2,1)S(1)}, u32[]{:S(2)}, u32[]{:S(2)}) %collective-permute-start.40) | collective-permute-done | bytes 344096 | tf_op jit(solution)/shard_map/ppermute | solution.py:137
  182.1 4.1 %fusion.84 = bf16[256,928]{0,1:T(8,128)(2,1)S(1)} fusion(bf16[256,2688]{1,0:T(8,128)(2,1)S(1)} %constant_dynamic-update-slice_fusion.31, bf16[1,2688,928]{1,2,0:T(8,128)(2,1)} %param.40), kind=kOutput, calls=%fused_computation.86 | convolution fusion | flops 1277878272 | bytes 6840320 | tf_op jit(solution)/shard_map/dot_general | solution.py:143
  186.3 1.7 fusion.25
  190.8 1.9 collective-permute-done.50
  194.4 1.7 fusion.28
  196.4 1.9 collective-permute-start.48
  201.2 2.4 %collective-permute-start.54 = (bf16[32,2688]{1,0:T(8,128)(2,1)S(1)}, bf16[32,2688]{1,0:T(8,128)(2,1)S(1)}, u32[]{:S(2)}, u32[]{:S(2)}) collective-permute-start(bf16[32,2688]{1,0:T(8,128)(2,1)S(1)} %get-tuple-element.245), channel_id=1, source_target_pairs={{0,6},{1,7},{2,4},{3,5},{4,2},{5,3},{6,0},{7,1},{8,14},{9,15},{10,... | collective-permute-start | bytes 516104 | tf_op jit(solution)/shard_map/ppermute | solution.py:137
  205.7 2.7 %collective-permute-done.47 = bf16[32,2688]{1,0:T(8,128)(2,1)S(1)} collective-permute-done((bf16[32,2688]{1,0:T(8,128)(2,1)S(1)}, bf16[32,2688]{1,0:T(8,128)(2,1)S(1)}, u32[]{:S(2)}, u32[]{:S(2)}) %collective-permute-start.47) | collective-permute-done | bytes 172064 | tf_op jit(solution)/shard_map/ppermute | solution.py:137
  210.1 1.9 collective-permute-start.49
  212.0 3.1 %collective-permute-done.53 = bf16[32,2688]{1,0:T(8,128)(2,1)S(1)} collective-permute-done((bf16[32,2688]{1,0:T(8,128)(2,1)S(1)}, bf16[32,2688]{1,0:T(8,128)(2,1)S(1)}, u32[]{:S(2)}, u32[]{:S(2)}) %collective-permute-start.53) | collective-permute-done | bytes 172064 | tf_op jit(solution)/shard_map/ppermute | solution.py:137
  215.7 9.6 %collective-permute-done.45 = bf16[64,2688]{1,0:T(8,128)(2,1)S(1)} collective-permute-done((bf16[64,2688]{1,0:T(8,128)(2,1)S(1)}, bf16[64,2688]{1,0:T(8,128)(2,1)S(1)}, u32[]{:S(2)}, u32[]{:S(2)}) %collective-permute-start.45) | collective-permute-done | bytes 344096 | tf_op jit(solution)/shard_map/ppermute | solution.py:137
  225.3 7.2 %collective-permute-done.55 = bf16[64,2688]{1,0:T(8,128)(2,1)S(1)} collective-permute-done((bf16[64,2688]{1,0:T(8,128)(2,1)S(1)}, bf16[64,2688]{1,0:T(8,128)(2,1)S(1)}, u32[]{:S(2)}, u32[]{:S(2)}) %collective-permute-start.55) | collective-permute-done | bytes 344096 | tf_op jit(solution)/shard_map/ppermute | solution.py:137
  (395 shorter events, 73.6 us)
Async XLA Ops:
  1.8 30.9 %collective-permute-start.7 = (bf16[160,1024]{1,0:T(8,128)(2,1)}, bf16[160,1024]{1,0:T(8,128)(2,1)}, u32[]{:S(2)}, u32[]{:S(2)}) collective-permute-start(bf16[160,1024]{1,0:T(8,128)(2,1)} %slice.561), channel_id=1, source_target_pairs={{0,4},{8,0},{16,8},{24,16},{28,24},{20,28},{12,20},{4,12},{1,5},{9... | collective-permute-start | bytes 983048 | tf_op jit(solution)/shard_map/ppermute | solution.py:25
  4.8 29.6 %collective-permute-start.5 = (bf16[160,1024]{1,0:T(8,128)(2,1)}, bf16[160,1024]{1,0:T(8,128)(2,1)}, u32[]{:S(2)}, u32[]{:S(2)}) collective-permute-start(bf16[160,1024]{1,0:T(8,128)(2,1)} %slice.561), channel_id=1, source_target_pairs={{0,8},{8,16},{16,24},{24,28},{28,20},{20,12},{12,4},{4,0},{1,9},{9... | collective-permute-start | bytes 983048 | tf_op jit(solution)/shard_map/ppermute | solution.py:25
  6.6 28.1 %collective-permute-start.6 = (bf16[176,1024]{1,0:T(8,128)(2,1)}, bf16[176,1024]{1,0:T(8,128)(2,1)}, u32[]{:S(2)}, u32[]{:S(2)}) collective-permute-start(bf16[176,1024]{1,0:T(8,128)(2,1)} %slice.560), channel_id=1, source_target_pairs={{0,4},{8,0},{16,8},{24,16},{28,24},{20,28},{12,20},{4,12},{1,5},{9... | collective-permute-start | bytes 1081352 | tf_op jit(solution)/shard_map/ppermute | solution.py:25
  8.6 27.9 %collective-permute-start.4 = (bf16[176,1024]{1,0:T(8,128)(2,1)}, bf16[176,1024]{1,0:T(8,128)(2,1)}, u32[]{:S(2)}, u32[]{:S(2)}) collective-permute-start(bf16[176,1024]{1,0:T(8,128)(2,1)} %slice.560), channel_id=1, source_target_pairs={{0,8},{8,16},{16,24},{24,28},{28,20},{20,12},{12,4},{4,0},{1,9},{9... | collective-permute-start | bytes 1081352 | tf_op jit(solution)/shard_map/ppermute | solution.py:25
  11.7 13.1 %collective-permute-start = (bf16[528,128]{1,0:T(8,128)(2,1)S(1)}, bf16[528,128]{1,0:T(8,128)(2,1)S(1)}, u32[]{:S(2)}, u32[]{:S(2)}) collective-permute-start(bf16[528,128]{1,0:T(8,128)(2,1)S(1)} %pad_maximum_fusion.10), channel_id=1, source_target_pairs={{0,4},{4,0},{8,12},{12,8},{16,20},{20,16},{24,28},{28,24},{1,5},{5... | collective-permute-start | bytes 405512 | tf_op jit(solution)/shard_map/ppermute | solution.py:54
  25.2 5.1 %collective-permute-start.1 = (bf16[528,128]{1,0:T(8,128)(2,1)S(1)}, bf16[528,128]{1,0:T(8,128)(2,1)S(1)}, u32[]{:S(2)}, u32[]{:S(2)}) collective-permute-start(bf16[528,128]{1,0:T(8,128)(2,1)S(1)} %pad_maximum_fusion.11), channel_id=1, source_target_pairs={{0,8},{4,12},{8,0},{12,4},{16,24},{20,28},{24,16},{28,20},{1,9},{5... | collective-permute-start | bytes 405512 | tf_op jit(solution)/shard_map/ppermute | solution.py:79
  31.6 8.7 %collective-permute-start.2 = (bf16[528,128]{1,0:T(8,128)(2,1)}, bf16[528,128]{1,0:T(8,128)(2,1)S(1)}, u32[]{:S(2)}, u32[]{:S(2)}) collective-permute-start(bf16[528,128]{1,0:T(8,128)(2,1)} %pad_maximum_fusion.12), channel_id=1, source_target_pairs={{0,16},{4,20},{8,24},{12,28},{16,0},{20,4},{24,8},{28,12},{1,17},{... | collective-permute-start | bytes 405512 | tf_op jit(solution)/shard_map/ppermute | solution.py:79
  32.7 29.1 %collective-permute-start.11 = (bf16[160,1024]{1,0:T(8,128)(2,1)}, bf16[160,1024]{1,0:T(8,128)(2,1)}, u32[]{:S(2)}, u32[]{:S(2)}) collective-permute-start(bf16[160,1024]{1,0:T(8,128)(2,1)} %collective-permute-done.7), channel_id=1, source_target_pairs={{0,4},{8,0},{16,8},{24,16},{28,24},{20,28},{12,20},{4,12},{1,5},{9... | collective-permute-start | bytes 983048 | tf_op jit(solution)/shard_map/ppermute | solution.py:25
  34.4 27.7 %collective-permute-start.9 = (bf16[160,1024]{1,0:T(8,128)(2,1)}, bf16[160,1024]{1,0:T(8,128)(2,1)}, u32[]{:S(2)}, u32[]{:S(2)}) collective-permute-start(bf16[160,1024]{1,0:T(8,128)(2,1)} %collective-permute-done.5), channel_id=1, source_target_pairs={{0,8},{8,16},{16,24},{24,28},{28,20},{20,12},{12,4},{4,0},{1,9},{9... | collective-permute-start | bytes 983048 | tf_op jit(solution)/shard_map/ppermute | solution.py:25
  34.7 29.1 %collective-permute-start.10 = (bf16[176,1024]{1,0:T(8,128)(2,1)}, bf16[176,1024]{1,0:T(8,128)(2,1)}, u32[]{:S(2)}, u32[]{:S(2)}) collective-permute-start(bf16[176,1024]{1,0:T(8,128)(2,1)} %collective-permute-done.6), channel_id=1, source_target_pairs={{0,4},{8,0},{16,8},{24,16},{28,24},{20,28},{12,20},{4,12},{1,5},{9... | collective-permute-start | bytes 1081352 | tf_op jit(solution)/shard_map/ppermute | solution.py:25
  36.5 27.3 %collective-permute-start.8 = (bf16[176,1024]{1,0:T(8,128)(2,1)}, bf16[176,1024]{1,0:T(8,128)(2,1)}, u32[]{:S(2)}, u32[]{:S(2)}) collective-permute-start(bf16[176,1024]{1,0:T(8,128)(2,1)} %collective-permute-done.4), channel_id=1, source_target_pairs={{0,8},{8,16},{16,24},{24,28},{28,20},{20,12},{12,4},{4,0},{1,9},{9... | collective-permute-start | bytes 1081352 | tf_op jit(solution)/shard_map/ppermute | solution.py:25
  40.5 11.5 %collective-permute-start.3 = (bf16[512,128]{1,0:T(8,128)(2,1)S(1)}, bf16[512,128]{1,0:T(8,128)(2,1)S(1)}, u32[]{:S(2)}, u32[]{:S(2)}) collective-permute-start(bf16[512,128]{1,0:T(8,128)(2,1)S(1)} %get-tuple-element.277), channel_id=1, source_target_pairs={{0,4},{4,0},{8,12},{12,8},{16,20},{20,16},{24,28},{28,24},{1,5},{5... | collective-permute-start | bytes 393224 | tf_op jit(solution)/shard_map/ppermute | solution.py:94
  61.7 11.0 %collective-permute-start.17 = (bf16[160,1024]{1,0:T(8,128)(2,1)}, bf16[160,1024]{1,0:T(8,128)(2,1)}, u32[]{:S(2)}, u32[]{:S(2)}) collective-permute-start(bf16[160,1024]{1,0:T(8,128)(2,1)} %collective-permute-done.11), channel_id=1, source_target_pairs={{0,4},{8,0},{16,8},{24,16},{28,24},{20,28},{12,20},{4,12},{1,5},{9... | collective-permute-start | bytes 983048 | tf_op jit(solution)/shard_map/ppermute | solution.py:25
  62.1 10.9 %collective-permute-start.15 = (bf16[160,1024]{1,0:T(8,128)(2,1)}, bf16[160,1024]{1,0:T(8,128)(2,1)}, u32[]{:S(2)}, u32[]{:S(2)}) collective-permute-start(bf16[160,1024]{1,0:T(8,128)(2,1)} %collective-permute-done.9), channel_id=1, source_target_pairs={{0,8},{8,16},{16,24},{24,28},{28,20},{20,12},{12,4},{4,0},{1,9},{9... | collective-permute-start | bytes 983048 | tf_op jit(solution)/shard_map/ppermute | solution.py:25
  66.1 13.6 %collective-permute-start.16 = (bf16[176,1024]{1,0:T(8,128)(2,1)}, bf16[176,1024]{1,0:T(8,128)(2,1)S(1)}, u32[]{:S(2)}, u32[]{:S(2)}) collective-permute-start(bf16[176,1024]{1,0:T(8,128)(2,1)} %collective-permute-done.10), channel_id=1, source_target_pairs={{0,4},{8,0},{16,8},{24,16},{28,24},{20,28},{12,20},{4,12},{1,5},{9... | collective-permute-start | bytes 1081352 | tf_op jit(solution)/shard_map/ppermute | solution.py:25
  66.4 13.3 %collective-permute-start.14 = (bf16[176,1024]{1,0:T(8,128)(2,1)}, bf16[176,1024]{1,0:T(8,128)(2,1)S(1)}, u32[]{:S(2)}, u32[]{:S(2)}) collective-permute-start(bf16[176,1024]{1,0:T(8,128)(2,1)} %collective-permute-done.8), channel_id=1, source_target_pairs={{0,8},{8,16},{16,24},{24,28},{28,20},{20,12},{12,4},{4,0},{1,9},{9... | collective-permute-start | bytes 1081352 | tf_op jit(solution)/shard_map/ppermute | solution.py:25
  68.4 13.7 %collective-permute-start.12 = (bf16[2,5,64,336]{3,2,1,0:T(8,128)(2,1)S(1)}, bf16[2,5,64,336]{3,2,1,0:T(8,128)(2,1)S(1)}, u32[]{:S(2)}, u32[]{:S(2)}) collective-permute-start(bf16[2,5,64,336]{3,2,1,0:T(8,128)(2,1)S(1)} %bitcast.327), channel_id=1, source_target_pairs={{0,1},{1,0},{2,3},{3,2},{4,5},{5,4},{6,7},{7,6},{8,9},{9,8},{10,11... | collective-permute-start | bytes 1290248 | tf_op jit(solution)/shard_map/ppermute | solution.py:129
  72.7 21.0 %collective-permute-start.21 = (bf16[160,1024]{1,0:T(8,128)(2,1)}, bf16[160,1024]{1,0:T(8,128)(2,1)}, u32[]{:S(2)}, u32[]{:S(2)}) collective-permute-start(bf16[160,1024]{1,0:T(8,128)(2,1)} %collective-permute-done.17), channel_id=1, source_target_pairs={{0,4},{8,0},{16,8},{24,16},{28,24},{20,28},{12,20},{4,12},{1,5},{9... | collective-permute-start | bytes 983048 | tf_op jit(solution)/shard_map/ppermute | solution.py:25
  81.9 11.8 %collective-permute-start.20 = (bf16[176,1024]{1,0:T(8,128)(2,1)S(1)}, bf16[176,1024]{1,0:T(8,128)(2,1)S(1)}, u32[]{:S(2)}, u32[]{:S(2)}) collective-permute-start(bf16[176,1024]{1,0:T(8,128)(2,1)S(1)} %collective-permute-done.14), channel_id=1, source_target_pairs={{0,8},{8,16},{16,24},{24,28},{28,20},{20,12},{12,4},{4,0},{1,9},{9... | collective-permute-start | bytes 1081352 | tf_op jit(solution)/shard_map/ppermute | solution.py:25
  83.4 5.7 %collective-permute-start.19 = (bf16[1,2,64,336]{3,2,1,0:T(8,128)(2,1)S(1)}, bf16[1,2,64,336]{3,2,1,0:T(8,128)(2,1)S(1)}, u32[]{:S(2)}, u32[]{:S(2)}) collective-permute-start(bf16[1,2,64,336]{3,2,1,0:T(8,128)(2,1)S(1)} %constant_dynamic-slice_fusion.1), channel_id=1, source_target_pairs={{0,2},{1,3},{2,0},{3,1},{4,6},{5,7},{6,4},{7,5},{8,10},{9,11},{10,... | collective-permute-start | bytes 258056 | tf_op jit(solution)/shard_map/ppermute | solution.py:129
  85.0 8.6 %collective-permute-start.13 = (bf16[1,5,64,336]{3,2,1,0:T(8,128)(2,1)S(1)}, bf16[1,5,64,336]{3,2,1,0:T(8,128)(2,1)S(1)}, u32[]{:S(2)}, u32[]{:S(2)}) collective-permute-start(bf16[1,5,64,336]{3,2,1,0:T(8,128)(2,1)S(1)} %constant_dynamic-slice_fusion.2), channel_id=1, source_target_pairs={{0,2},{1,3},{2,0},{3,1},{4,6},{5,7},{6,4},{7,5},{8,10},{9,11},{10,... | collective-permute-start | bytes 645128 | tf_op jit(solution)/shard_map/ppermute | solution.py:129
  103.3 17.1 %collective-permute-start.24 = (bf16[64,2816]{1,0:T(8,128)(2,1)S(1)}, bf16[64,2816]{1,0:T(8,128)(2,1)S(1)}, u32[]{:S(2)}, u32[]{:S(2)}) collective-permute-start(bf16[64,2816]{1,0:T(8,128)(2,1)S(1)} %fusion.145), channel_id=1, source_target_pairs={{0,16},{1,17},{2,18},{3,19},{4,20},{5,21},{6,22},{7,23},{8,24},{9,... | collective-permute-start | bytes 1081352 | tf_op jit(solution)/shard_map/ppermute | solution.py:137
  103.8 7.0 %collective-permute-start.25 = (bf16[32,2688]{1,0:T(8,128)(2,1)S(1)}, bf16[32,2688]{1,0:T(8,128)(2,1)S(1)}, u32[]{:S(2)}, u32[]{:S(2)}) collective-permute-start(bf16[32,2688]{1,0:T(8,128)(2,1)S(1)} %convolution_convert_fusion.17), channel_id=1, source_target_pairs={{0,2},{1,3},{2,0},{3,1},{4,6},{5,7},{6,4},{7,5},{8,10},{9,11},{10,... | collective-permute-start | bytes 516104 | tf_op jit(solution)/shard_map/ppermute | solution.py:137
  105.3 8.7 %collective-permute-start.26 = (bf16[32,2688]{1,0:T(8,128)(2,1)S(1)}, bf16[32,2688]{1,0:T(8,128)(2,1)S(1)}, u32[]{:S(2)}, u32[]{:S(2)}) collective-permute-start(bf16[32,2688]{1,0:T(8,128)(2,1)S(1)} %convolution_convert_fusion.16), channel_id=1, source_target_pairs={{0,4},{1,5},{2,6},{3,7},{4,0},{5,1},{6,2},{7,3},{8,12},{9,13},{10,... | collective-permute-start | bytes 516104 | tf_op jit(solution)/shard_map/ppermute | solution.py:137
  106.4 7.6 %collective-permute-start.27 = (bf16[32,2688]{1,0:T(8,128)(2,1)S(1)}, bf16[32,2688]{1,0:T(8,128)(2,1)S(1)}, u32[]{:S(2)}, u32[]{:S(2)}) collective-permute-start(bf16[32,2688]{1,0:T(8,128)(2,1)S(1)} %convolution_convert_fusion.15), channel_id=1, source_target_pairs={{0,6},{1,7},{2,4},{3,5},{4,2},{5,3},{6,0},{7,1},{8,14},{9,15},{10,... | collective-permute-start | bytes 516104 | tf_op jit(solution)/shard_map/ppermute | solution.py:137
  129.2 6.8 %collective-permute-start.33 = (bf16[128,2688]{1,0:T(8,128)(2,1)S(1)}, bf16[128,2688]{1,0:T(8,128)(2,1)S(1)}, u32[]{:S(2)}, u32[]{:S(2)}) collective-permute-start(bf16[128,2688]{1,0:T(8,128)(2,1)S(1)} %slice.592), channel_id=1, source_target_pairs={{0,1},{1,0},{2,3},{3,2},{4,5},{5,4},{6,7},{7,6},{8,9},{9,8},{10,11... | collective-permute-start | bytes 2064392 | tf_op jit(solution)/shard_map/ppermute | solution.py:137
  129.8 14.6 %collective-permute-start.28 = (bf16[64,2816]{1,0:T(8,128)(2,1)S(1)}, bf16[64,2816]{1,0:T(8,128)(2,1)S(1)}, u32[]{:S(2)}, u32[]{:S(2)}) collective-permute-start(bf16[64,2816]{1,0:T(8,128)(2,1)S(1)} %fusion.145), channel_id=1, source_target_pairs={{0,24},{1,25},{2,26},{3,27},{4,28},{5,29},{6,30},{7,31},{8,16},{9,... | collective-permute-start | bytes 1081352 | tf_op jit(solution)/shard_map/ppermute | solution.py:137
  131.8 7.2 %collective-permute-start.29 = (bf16[32,2688]{1,0:T(8,128)(2,1)S(1)}, bf16[32,2688]{1,0:T(8,128)(2,1)S(1)}, u32[]{:S(2)}, u32[]{:S(2)}) collective-permute-start(bf16[32,2688]{1,0:T(8,128)(2,1)S(1)} %convolution_convert_fusion.13), channel_id=1, source_target_pairs={{0,2},{1,3},{2,0},{3,1},{4,6},{5,7},{6,4},{7,5},{8,10},{9,11},{10,... | collective-permute-start | bytes 516104 | tf_op jit(solution)/shard_map/ppermute | solution.py:137
  133.3 9.8 %collective-permute-start.30 = (bf16[32,2688]{1,0:T(8,128)(2,1)S(1)}, bf16[32,2688]{1,0:T(8,128)(2,1)S(1)}, u32[]{:S(2)}, u32[]{:S(2)}) collective-permute-start(bf16[32,2688]{1,0:T(8,128)(2,1)S(1)} %convolution_convert_fusion.12), channel_id=1, source_target_pairs={{0,4},{1,5},{2,6},{3,7},{4,0},{5,1},{6,2},{7,3},{8,12},{9,13},{10,... | collective-permute-start | bytes 516104 | tf_op jit(solution)/shard_map/ppermute | solution.py:137
  134.6 8.4 %collective-permute-start.31 = (bf16[32,2688]{1,0:T(8,128)(2,1)S(1)}, bf16[32,2688]{1,0:T(8,128)(2,1)S(1)}, u32[]{:S(2)}, u32[]{:S(2)}) collective-permute-start(bf16[32,2688]{1,0:T(8,128)(2,1)S(1)} %convolution_convert_fusion.11), channel_id=1, source_target_pairs={{0,6},{1,7},{2,4},{3,5},{4,2},{5,3},{6,0},{7,1},{8,14},{9,15},{10,... | collective-permute-start | bytes 516104 | tf_op jit(solution)/shard_map/ppermute | solution.py:137
  145.8 23.3 %collective-permute-start.34 = (bf16[64,2816]{1,0:T(8,128)(2,1)}, bf16[64,2816]{1,0:T(8,128)(2,1)S(1)}, u32[]{:S(2)}, u32[]{:S(2)}) collective-permute-start(bf16[64,2816]{1,0:T(8,128)(2,1)} %copy-done.15), channel_id=1, source_target_pairs={{0,8},{1,9},{2,10},{3,11},{4,12},{5,13},{6,14},{7,15},{8,0},{9,1},... | collective-permute-start | bytes 1081352 | tf_op jit(solution)/shard_map/ppermute | solution.py:137
  149.7 11.0 %collective-permute-start.35 = (bf16[64,2688]{1,0:T(8,128)(2,1)S(1)}, bf16[64,2688]{1,0:T(8,128)(2,1)S(1)}, u32[]{:S(2)}, u32[]{:S(2)}) collective-permute-start(bf16[64,2688]{1,0:T(8,128)(2,1)S(1)} %pad_maximum_fusion.4), channel_id=1, source_target_pairs={{0,2},{1,3},{2,0},{3,1},{4,6},{5,7},{6,4},{7,5},{8,10},{9,11},{10,... | collective-permute-start | bytes 1032200 | tf_op jit(solution)/shard_map/ppermute | solution.py:137
  151.2 16.4 %collective-permute-start.36 = (bf16[64,2688]{1,0:T(8,128)(2,1)S(1)}, bf16[64,2688]{1,0:T(8,128)(2,1)S(1)}, u32[]{:S(2)}, u32[]{:S(2)}) collective-permute-start(bf16[64,2688]{1,0:T(8,128)(2,1)S(1)} %pad_maximum_fusion.5), channel_id=1, source_target_pairs={{0,4},{1,5},{2,6},{3,7},{4,0},{5,1},{6,2},{7,3},{8,12},{9,13},{10,... | collective-permute-start | bytes 1032200 | tf_op jit(solution)/shard_map/ppermute | solution.py:137
  152.4 15.9 %collective-permute-start.37 = (bf16[64,2688]{1,0:T(8,128)(2,1)S(1)}, bf16[64,2688]{1,0:T(8,128)(2,1)S(1)}, u32[]{:S(2)}, u32[]{:S(2)}) collective-permute-start(bf16[64,2688]{1,0:T(8,128)(2,1)S(1)} %pad_maximum_fusion.6), channel_id=1, source_target_pairs={{0,6},{1,7},{2,4},{3,5},{4,2},{5,3},{6,0},{7,1},{8,14},{9,15},{10,... | collective-permute-start | bytes 1032200 | tf_op jit(solution)/shard_map/ppermute | solution.py:137
  153.6 7.1 %collective-permute-start.38 = (bf16[128,2688]{1,0:T(8,128)(2,1)S(1)}, bf16[128,2688]{1,0:T(8,128)(2,1)S(1)}, u32[]{:S(2)}, u32[]{:S(2)}) collective-permute-start(bf16[128,2688]{1,0:T(8,128)(2,1)S(1)} %pad_maximum_fusion.1), channel_id=1, source_target_pairs={{0,1},{1,0},{2,3},{3,2},{4,5},{5,4},{6,7},{7,6},{8,9},{9,8},{10,11... | collective-permute-start | bytes 2064392 | tf_op jit(solution)/shard_map/ppermute | solution.py:137
  171.0 11.0 %collective-permute-start.40 = (bf16[64,2688]{1,0:T(8,128)(2,1)S(1)}, bf16[64,2688]{1,0:T(8,128)(2,1)S(1)}, u32[]{:S(2)}, u32[]{:S(2)}) collective-permute-start(bf16[64,2688]{1,0:T(8,128)(2,1)S(1)} %pad_maximum_fusion.7), channel_id=1, source_target_pairs={{0,2},{1,3},{2,0},{3,1},{4,6},{5,7},{6,4},{7,5},{8,10},{9,11},{10,... | collective-permute-start | bytes 1032200 | tf_op jit(solution)/shard_map/ppermute | solution.py:137
  172.5 17.3 %collective-permute-start.41 = (bf16[64,2688]{1,0:T(8,128)(2,1)S(1)}, bf16[64,2688]{1,0:T(8,128)(2,1)S(1)}, u32[]{:S(2)}, u32[]{:S(2)}) collective-permute-start(bf16[64,2688]{1,0:T(8,128)(2,1)S(1)} %pad_maximum_fusion.8), channel_id=1, source_target_pairs={{0,4},{1,5},{2,6},{3,7},{4,0},{5,1},{6,2},{7,3},{8,12},{9,13},{10,... | collective-permute-start | bytes 1032200 | tf_op jit(solution)/shard_map/ppermute | solution.py:137
  173.7 16.1 %collective-permute-start.42 = (bf16[64,2688]{1,0:T(8,128)(2,1)S(1)}, bf16[64,2688]{1,0:T(8,128)(2,1)S(1)}, u32[]{:S(2)}, u32[]{:S(2)}) collective-permute-start(bf16[64,2688]{1,0:T(8,128)(2,1)S(1)} %pad_maximum_fusion.9), channel_id=1, source_target_pairs={{0,6},{1,7},{2,4},{3,5},{4,2},{5,3},{6,0},{7,1},{8,14},{9,15},{10,... | collective-permute-start | bytes 1032200 | tf_op jit(solution)/shard_map/ppermute | solution.py:137
  174.9 7.1 %collective-permute-start.43 = (bf16[128,2688]{1,0:T(8,128)(2,1)S(1)}, bf16[128,2688]{1,0:T(8,128)(2,1)S(1)}, u32[]{:S(2)}, u32[]{:S(2)}) collective-permute-start(bf16[128,2688]{1,0:T(8,128)(2,1)S(1)} %pad_maximum_fusion.2), channel_id=1, source_target_pairs={{0,1},{1,0},{2,3},{3,2},{4,5},{5,4},{6,7},{7,6},{8,9},{9,8},{10,11... | collective-permute-start | bytes 2064392 | tf_op jit(solution)/shard_map/ppermute | solution.py:137
  196.4 8.3 %collective-permute-start.48 = (bf16[32,2688]{1,0:T(8,128)(2,1)S(1)}, bf16[32,2688]{1,0:T(8,128)(2,1)S(1)}, u32[]{:S(2)}, u32[]{:S(2)}) collective-permute-start(bf16[32,2688]{1,0:T(8,128)(2,1)S(1)} %get-tuple-element.241), channel_id=1, source_target_pairs={{0,6},{1,7},{2,4},{3,5},{4,2},{5,3},{6,0},{7,1},{8,14},{9,15},{10,... | collective-permute-start | bytes 516104 | tf_op jit(solution)/shard_map/ppermute | solution.py:137
  198.4 10.0 %collective-permute-start.47 = (bf16[32,2688]{1,0:T(8,128)(2,1)S(1)}, bf16[32,2688]{1,0:T(8,128)(2,1)S(1)}, u32[]{:S(2)}, u32[]{:S(2)}) collective-permute-start(bf16[32,2688]{1,0:T(8,128)(2,1)S(1)} %get-tuple-element.242), channel_id=1, source_target_pairs={{0,4},{1,5},{2,6},{3,7},{4,0},{5,1},{6,2},{7,3},{8,12},{9,13},{10,... | collective-permute-start | bytes 516104 | tf_op jit(solution)/shard_map/ppermute | solution.py:137
  199.3 10.5 %collective-permute-start.46 = (bf16[32,2688]{1,0:T(8,128)(2,1)S(1)}, bf16[32,2688]{1,0:T(8,128)(2,1)S(1)}, u32[]{:S(2)}, u32[]{:S(2)}) collective-permute-start(bf16[32,2688]{1,0:T(8,128)(2,1)S(1)} %get-tuple-element.243), channel_id=1, source_target_pairs={{0,2},{1,3},{2,0},{3,1},{4,6},{5,7},{6,4},{7,5},{8,10},{9,11},{10,... | collective-permute-start | bytes 516104 | tf_op jit(solution)/shard_map/ppermute | solution.py:137
  200.2 25.1 %collective-permute-start.45 = (bf16[64,2688]{1,0:T(8,128)(2,1)S(1)}, bf16[64,2688]{1,0:T(8,128)(2,1)S(1)}, u32[]{:S(2)}, u32[]{:S(2)}) collective-permute-start(bf16[64,2688]{1,0:T(8,128)(2,1)S(1)} %convolution_convert_fusion.2), channel_id=1, source_target_pairs={{0,16},{1,17},{2,18},{3,19},{4,20},{5,21},{6,22},{7,23},{8,24},{9,... | collective-permute-start | bytes 1032200 | tf_op jit(solution)/shard_map/ppermute | solution.py:137
  201.2 10.8 %collective-permute-start.54 = (bf16[32,2688]{1,0:T(8,128)(2,1)S(1)}, bf16[32,2688]{1,0:T(8,128)(2,1)S(1)}, u32[]{:S(2)}, u32[]{:S(2)}) collective-permute-start(bf16[32,2688]{1,0:T(8,128)(2,1)S(1)} %get-tuple-element.245), channel_id=1, source_target_pairs={{0,6},{1,7},{2,4},{3,5},{4,2},{5,3},{6,0},{7,1},{8,14},{9,15},{10,... | collective-permute-start | bytes 516104 | tf_op jit(solution)/shard_map/ppermute | solution.py:137
  204.7 10.4 %collective-permute-start.53 = (bf16[32,2688]{1,0:T(8,128)(2,1)S(1)}, bf16[32,2688]{1,0:T(8,128)(2,1)S(1)}, u32[]{:S(2)}, u32[]{:S(2)}) collective-permute-start(bf16[32,2688]{1,0:T(8,128)(2,1)S(1)} %get-tuple-element.246), channel_id=1, source_target_pairs={{0,4},{1,5},{2,6},{3,7},{4,0},{5,1},{6,2},{7,3},{8,12},{9,13},{10,... | collective-permute-start | bytes 516104 | tf_op jit(solution)/shard_map/ppermute | solution.py:137
  208.4 6.7 %collective-permute-start.52 = (bf16[32,2688]{1,0:T(8,128)(2,1)S(1)}, bf16[32,2688]{1,0:T(8,128)(2,1)S(1)}, u32[]{:S(2)}, u32[]{:S(2)}) collective-permute-start(bf16[32,2688]{1,0:T(8,128)(2,1)S(1)} %get-tuple-element.247), channel_id=1, source_target_pairs={{0,2},{1,3},{2,0},{3,1},{4,6},{5,7},{6,4},{7,5},{8,10},{9,11},{10,... | collective-permute-start | bytes 516104 | tf_op jit(solution)/shard_map/ppermute | solution.py:137
  210.1 15.2 %collective-permute-start.49 = (bf16[64,2688]{1,0:T(8,128)(2,1)S(1)}, bf16[64,2688]{1,0:T(8,128)(2,1)S(1)}, u32[]{:S(2)}, u32[]{:S(2)}) collective-permute-start(bf16[64,2688]{1,0:T(8,128)(2,1)S(1)} %convolution_convert_fusion.1), channel_id=1, source_target_pairs={{0,24},{1,25},{2,26},{3,27},{4,28},{5,29},{6,30},{7,31},{8,16},{9,... | collective-permute-start | bytes 1032200 | tf_op jit(solution)/shard_map/ppermute | solution.py:137
  215.4 17.2 %collective-permute-start.55 = (bf16[64,2688]{1,0:T(8,128)(2,1)S(1)}, bf16[64,2688]{1,0:T(8,128)(2,1)S(1)}, u32[]{:S(2)}, u32[]{:S(2)}) collective-permute-start(bf16[64,2688]{1,0:T(8,128)(2,1)S(1)} %convolution_convert_fusion), channel_id=1, source_target_pairs={{0,8},{1,9},{2,10},{3,11},{4,12},{5,13},{6,14},{7,15},{8,0},{9,1},... | collective-permute-start | bytes 1032200 | tf_op jit(solution)/shard_map/ppermute | solution.py:137
  (51 other events, 211.9 us)
